TPU v7x, 32 devices: a whole 2x2x4 slice. The times are simulated.
32 devices in a mesh: sub: 4 (over x, core), slab: 8 (over z, y).
Axes of the slice: x: 2, y: 2, z: 4, core: 2. Of those that a mesh axis runs over, the one named last changes fastest.
Arguments:
- source: float32 [4, 256, 256, 256], P('sub', 'slab'), may hold values from -6 to 6
- coarse: float32 [2, 4, 256, 256, 256], P(None, 'sub', 'slab'), may hold values from -4 to 4
- rho: float32 [4], replicated, may hold values from 0.3 to 45, as said below
- basis_x: float32 [256, 256], replicated, may hold values from -0.375 to 0.375
- basis_y: float32 [256, 256], replicated, may hold values from -0.375 to 0.375
- basis_z: float32 [256, 256], replicated, may hold values from -0.375 to 0.375
- eigen_x: float32 [256], replicated, may hold values from 0.1 to 3
- eigen_y: float32 [256], replicated, may hold values from 0.1 to 3
- eigen_z: float32 [256], replicated, may hold values from 0.1 to 3
- face_stiff: float32 [256, 256], replicated, may hold values from 0.2 to 2
Outputs:
- solution: float32 [4, 256, 256, 256], P('sub', 'slab')
- multipliers: float32 [4, 256, 256], P('sub', 'slab')
- jump: float32 [4, 256, 256], P('sub', 'slab')
Inputs may be any that keep to these rules, and one draw needn't show every extreme that they name: `rho`: positive coefficient of each subdomain.
All inputs are finite; a program needn't handle non-finite values.
Results may differ from a plain program's by a relative error of at most 0.00014.
Values sent between devices are 32-bit elements; how exact they have to be, the bound alone decides.
A program may use at most 128 MiB of HBM per device.

v0:
```python
import jax
import jax.numpy as jnp
from jax import lax
from jax.sharding import PartitionSpec as P

ITERS = 2


HI = lax.Precision.HIGHEST


def from_behind(block, axis, distance):
    devices = range(lax.axis_size(axis))
    route = [((i - distance) % len(devices), i) for i in devices]
    return lax.ppermute(block, axis, route)


def volume_tail(spread, basis_y, basis_z):
    slabs = lax.all_to_all(spread, "slab", split_axis=0, concat_axis=1, tiled=True)
    part = jnp.einsum("xjk,yj->xyk", slabs, basis_y, precision=HI)
    return jnp.einsum("xyk,zk->xyz", part, basis_z, precision=HI)


def on_device(
    source, coarse, rho, basis_x, basis_y, basis_z, eigen_x, eigen_y, eigen_z, face_stiff
):
    field = source[0]
    rows = field.shape[0]
    width = field.shape[1]
    sub_index = lax.axis_index("sub")
    slab_index = lax.axis_index("slab")
    subs = lax.axis_size("sub")
    own_rho = lax.dynamic_slice_in_dim(rho, sub_index, 1, 0)[0]
    next_rho = lax.dynamic_slice_in_dim(rho, (sub_index + 1) % subs, 1, 0)[0]
    weight = 0.5 * (own_rho + next_rho)
    start = slab_index * rows
    eigen_part = lax.dynamic_slice_in_dim(eigen_y, start, rows, 0)
    stiff_part = lax.dynamic_slice_in_dim(face_stiff, start, rows, 1)
    denom = (eigen_x[:, None, None] + eigen_part[None, :, None] + eigen_z[None, None, :]) * own_rho
    edge_basis = jnp.stack([basis_z[0], basis_z[width - 1]])
    multipliers = jnp.zeros((rows, width), jnp.float32)
    solution = field
    jump = multipliers
    for step in range(ITERS):
        earlier = from_behind(multipliers, "sub", 1)
        load = field + coarse[step, 0]
        load = load.at[:, :, width - 1].add(-multipliers)
        load = load.at[:, :, 0].add(earlier)
        part = jnp.einsum("xyz,zk->xyk", load, basis_z, precision=HI)
        part = jnp.einsum("xyk,yj->xjk", part, basis_y, precision=HI)
        lines = lax.all_to_all(part, "slab", split_axis=1, concat_axis=0, tiled=True)
        modes = jnp.einsum("xjk,xi->ijk", lines, basis_x, precision=HI) / denom
        spread = jnp.einsum("ijk,xi->xjk", modes, basis_x, precision=HI)
        edges = jnp.einsum("xjk,pk->pxj", spread, edge_basis, precision=HI)
        edges = lax.all_to_all(edges, "slab", split_axis=1, concat_axis=2, tiled=True)
        edges = jnp.einsum("pxj,yj->pxy", edges, basis_y, precision=HI)
        first = edges[0]
        last = edges[1]
        if step == ITERS - 1:
            solution = volume_tail(spread, basis_y, basis_z)
        following = from_behind(first, "sub", -1)
        jump = last - following
        face = jnp.dot(jump, basis_y, precision=HI, preferred_element_type=jnp.float32)
        face = lax.all_to_all(face, "slab", split_axis=1, concat_axis=0, tiled=True)
        face = jnp.einsum("xj,xi->ij", face, basis_x, precision=HI) * stiff_part
        face = jnp.einsum("ij,xi->xj", face, basis_x, precision=HI)
        face = lax.all_to_all(face, "slab", split_axis=0, concat_axis=1, tiled=True)
        face = jnp.einsum("xj,yj->xy", face, basis_y, precision=HI)
        search = weight * face
        upper, lower = lax.psum((jnp.sum(jump * search), jnp.sum(search * search)), ("sub", "slab"))
        alpha = upper / (lower + 1e-06)
        multipliers = multipliers + alpha * search
    return (solution[None], multipliers[None], jump[None])


def solution(mesh):
    in_specs = (
        P("sub", "slab", None, None),
        P(None, "sub", "slab", None, None),
        P(),
        P(),
        P(),
        P(),
        P(),
        P(),
        P(),
        P(),
    )
    out_specs = (P("sub", "slab", None, None), P("sub", "slab", None), P("sub", "slab", None))
    return jax.shard_map(
        on_device, mesh=mesh, in_specs=in_specs, out_specs=out_specs, check_vma=False
    )
```

profile of v0, /device:TPU:0, one launch (start us, length us, event | category | flops | bytes accessed | tf_op | source)
XLA Modules:
  0.0 953.6 jit_solution(14270782941773032381)
XLA Ops:
  1.2 11.3 %fusion.55 = (f32[1,1,32,256,256]{4,3,2,1,0:T(8,128)}, f32[1,1,32,256,256]{4,3,2,1,0:T(8,128)}) fusion(f32[2,1,32,256,256]{4,3,2,1,0:T(8,128)} %param.19), kind=kLoop, calls=%fused_computation.83 | loop fusion | bytes 33554432 | tf_op jit(solution)/shard_map/slice | solution.py:46
  12.5 10.3 %copy.116 = f32[1,1,32,256,256]{3,2,4,1,0:T(8,128)} copy(f32[1,1,32,256,256]{4,3,2,1,0:T(8,128)} %get-tuple-element.61) | data formatting | bytes 16777216
  22.8 10.2 %copy.69 = f32[1,32,256,256]{2,1,3,0:T(8,128)} copy(f32[1,32,256,256]{3,2,1,0:T(8,128)} %param.18) | data formatting | bytes 16777216 | tf_op args[0]
  33.0 10.3 %copy.115 = f32[1,1,32,256,256]{3,2,4,1,0:T(8,128)} copy(f32[1,1,32,256,256]{4,3,2,1,0:T(8,128)} %get-tuple-element.62) | data formatting | bytes 16777216
  43.3 13.9 %bitcast_add_fusion = (f32[32,256,256]{1,0,2:T(8,128)S(1)}, f32[32,256,256]{1,0,2:T(8,128)}) fusion(f32[1,1,32,256,256]{3,2,4,1,0:T(8,128)} %copy.116, f32[1,32,256,256]{2,1,3,0:T(8,128)} %copy.69, f32[1,1,32,256,256]{3,2,4,1,0:T(8,128)} %copy.115), kind=kLoop, calls=%fused_computation.8 | loop fusion | flops 4194304 | bytes 41943040 | tf_op jit(solution)/shard_map/add | solution.py:46
  57.3 13.9 %fusion.12 = f32[32,256,256]{1,2,0:T(8,128)S(1)} fusion(f32[32,256,256]{1,0,2:T(8,128)S(1)} %fusion.44, f32[256,256]{1,0:T(8,128)S(1)} %copy-done.3), kind=kOutput, calls=%fused_computation.16 | convolution fusion | flops 6442450944 | bytes 17039360 | tf_op jit(solution)/shard_map/xyz,zk->xyk/dot_general | solution.py:49
  71.2 8.8 convolution_bitcast_fusion.1
  80.0 10.3 %copy.74 = f32[32,256,256]{2,0,1:T(8,128)} copy(f32[32,256,256]{1,2,0:T(8,128)} %convolution_bitcast_fusion.1) | data formatting | bytes 16777216 | tf_op jit(solution)/shard_map/xyk,yj->xjk/transpose | solution.py:50
  90.3 7.0 all-to-all-start
  98.0 183.9 %all-to-all-done = f32[32,256,256]{2,0,1:T(8,128)} async-done(((f32[32,256,256]{2,0,1:T(8,128)}), f32[32,256,256]{2,0,1:T(8,128)}, u32[]{:S(2)}, u32[]{:S(2)}) %all-to-all-start) | async-done | bytes 8388640 | tf_op jit(solution)/shard_map/all_to_all | solution.py:51
  281.9 8.1 copy.76
  290.1 17.7 %fusion.10 = f32[32,256,256]{2,1,0:T(8,128)S(1)} fusion(f32[256,32,256]{2,1,0:T(8,128)S(1)} %bitcast.174, f32[256,256]{1,0:T(8,128)S(1)} %copy-done), kind=kOutput, calls=%fused_computation.14 | convolution fusion | flops 6442450944 | bytes 17039360 | tf_op jit(solution)/shard_map/xjk,xi->ijk/dot_general | solution.py:52
  307.8 8.6 fusion.5
  316.5 4.0 fusion.3
  320.9 10.3 %all_to_all.166 = f32[8,1,2048]{2,1,0:T(1,128)S(1)} all-to-all(f32[8,1,2048]{2,1,0:T(1,128)S(1)} %reshape.173), channel_id=1, replica_groups=mesh['sub'=4,'slab'=8] {'slab'}, dimensions={0} | all-to-all | bytes 131072 | tf_op jit(solution)/shard_map/all_to_all | solution.py:55
  331.8 0.8 reduce.8
  333.8 1.6 collective-permute-done.1
  336.7 3.3 all-to-all-start.2
  340.3 6.6 all-to-all-done.2
  346.9 0.8 reduce.9
  349.4 3.3 all-to-all-start.3
  353.9 5.4 all-to-all-done.3
  360.4 1.0 multiply_reduce_fusion.2
  361.3 38.3 %all-reduce.1 = (f32[]{:T(128)}, f32[]{:T(128)}) all-reduce(f32[]{:T(128)} %get-tuple-element.54, f32[]{:T(128)} %get-tuple-element.53), channel_id=1, replica_groups=mesh['sub'=4,'slab'=8] {'sub','slab'}, use_global_device_ids=true, to_apply=%region_1.2 | all-reduce | flops 2 | bytes 16 | tf_op jit(solution)/shard_map/psum | solution.py:70
  400.9 1.4 fusion.46
  402.3 3.3 collective-permute-done.2
  405.6 1.4 fusion.42
  407.0 15.9 %fusion.8 = f32[32,256,256]{1,2,0:T(8,128)S(1)} fusion(f32[32,256,256]{1,0,2:T(8,128)} %fusion.42, f32[256,256]{1,0:T(8,128)S(1)} %copy-done.3), kind=kOutput, calls=%fused_computation.12 | convolution fusion | flops 6442450944 | bytes 17039360 | tf_op jit(solution)/shard_map/xyz,zk->xyk/dot_general | solution.py:49
  422.9 8.9 convolution_bitcast_fusion
  431.9 10.3 %copy.88 = f32[32,256,256]{2,0,1:T(8,128)} copy(f32[32,256,256]{1,2,0:T(8,128)} %convolution_bitcast_fusion) | data formatting | bytes 16777216 | tf_op jit(solution)/shard_map/xyk,yj->xjk/transpose | solution.py:50
  442.2 187.7 %all_to_all.167 = f32[32,256,256]{2,0,1:T(8,128)S(1)} all-to-all(f32[32,256,256]{2,0,1:T(8,128)} %copy.88), channel_id=1, replica_groups=mesh['sub'=4,'slab'=8] {'slab'}, dimensions={1} | all-to-all | bytes 16777216 | tf_op jit(solution)/shard_map/all_to_all | solution.py:51
  629.8 4.8 copy.90
  634.7 17.7 %fusion.6 = f32[32,256,256]{2,1,0:T(8,128)S(1)} fusion(f32[256,32,256]{2,1,0:T(8,128)S(1)} %bitcast.176, f32[256,256]{1,0:T(8,128)S(1)} %copy-done), kind=kOutput, calls=%fused_computation.10 | convolution fusion | flops 6442450944 | bytes 17039360 | tf_op jit(solution)/shard_map/xjk,xi->ijk/dot_general | solution.py:52
  652.4 8.6 fusion.20
  661.1 3.4 copy-done.1
  664.5 4.0 fusion.49
  668.9 10.0 %all_to_all.168 = f32[8,1,2048]{2,1,0:T(1,128)S(1)} all-to-all(f32[8,1,2048]{2,1,0:T(1,128)S(1)} %reshape.179), channel_id=1, replica_groups=mesh['sub'=4,'slab'=8] {'slab'}, dimensions={0} | all-to-all | bytes 131072 | tf_op jit(solution)/shard_map/all_to_all | solution.py:55
  678.9 0.8 reduce.11
  680.7 1.6 collective-permute-done.3
  683.0 9.1 all_to_all.169
  694.6 3.3 all-to-all-start.8
  698.0 10.3 %copy.92 = f32[256,32,256]{2,1,0:T(8,128)} copy(f32[256,32,256]{0,2,1:T(8,128)} %copy-done.1) | data formatting | bytes 16777216 | tf_op jit(solution)/shard_map/ijk,xi->xjk/dot_general | solution.py:53
  708.3 5.9 all-to-all-start.5
  715.6 1.2 multiply_reduce_fusion
  716.8 200.2 %all-reduce = (f32[]{:T(128)}, f32[]{:T(128)}) all-reduce(f32[]{:T(128)} %get-tuple-element.52, f32[]{:T(128)} %get-tuple-element.51), channel_id=1, replica_groups=mesh['sub'=4,'slab'=8] {'sub','slab'}, use_global_device_ids=true, to_apply=%region_5.6 | all-reduce | flops 2 | bytes 16 | tf_op jit(solution)/shard_map/psum | solution.py:70
  919.0 4.3 copy.93
  923.2 14.3 %fusion.32 = f32[32,256,256]{2,1,0:T(8,128)S(1)} fusion(f32[32,256,256]{2,1,0:T(8,128)S(1)} %bitcast.177, f32[256,256]{1,0:T(8,128)S(1)} %copy-done.2), kind=kOutput, calls=%fused_computation.43 | convolution fusion | flops 6442450944 | bytes 17039360 | tf_op jit(solution)/shard_map/xjk,yj->xyk/dot_general | solution.py:20
  937.5 15.9 %fusion.21 = f32[1,32,256,256]{3,2,1,0:T(8,128)} fusion(f32[32,256,256]{2,1,0:T(8,128)S(1)} %fusion.32, f32[256,256]{1,0:T(8,128)S(1)} %copy-done.3), kind=kOutput, calls=%fused_computation.26 | convolution fusion | flops 6442450944 | bytes 17039360 | tf_op jit(solution)/shard_map/xyk,zk->xyz/dot_general | solution.py:21
  (79 shorter events, 14.2 us)
Async XLA Ops:
  0.6 289.4 %copy-start = (f32[256,256]{1,0:T(8,128)S(1)}, f32[256,256]{1,0:T(8,128)}, u32[]{:S(2)}) copy-start(f32[256,256]{1,0:T(8,128)} %param.21) | copy-start | bytes 786436
  0.7 56.6 %collective-permute-start = (f32[32,256]{1,0:T(8,128)S(1)}, f32[32,256]{1,0:T(8,128)S(1)}, u32[]{:S(2)}, u32[]{:S(2)}) collective-permute-start(f32[32,256]{1,0:T(8,128)S(1)} %broadcast_in_dim.15), channel_id=1, source_target_pairs={{24,0},{0,8},{8,16},{16,24},{25,1},{1,9},{9,17},{17,25},{26,2},{2,... | collective-permute-start | bytes 98312 | tf_op jit(solution)/shard_map/ppermute | solution.py:15
  43.3 13.9 %copy-start.3 = (f32[256,256]{1,0:T(8,128)S(1)}, f32[256,256]{1,0:T(8,128)}, u32[]{:S(2)}) copy-start(f32[256,256]{1,0:T(8,128)} %param.23) | copy-start | bytes 786436
  57.3 13.9 %copy-start.2 = (f32[256,256]{1,0:T(8,128)S(1)}, f32[256,256]{1,0:T(8,128)}, u32[]{:S(2)}) copy-start(f32[256,256]{1,0:T(8,128)} %param.22) | copy-start | bytes 786436
  90.3 7.0 copy-start.7
  90.3 7.1 copy-start.5
  90.3 7.7 copy-start.6
  90.3 191.6 %all-to-all-start = ((f32[32,256,256]{2,0,1:T(8,128)}), f32[32,256,256]{2,0,1:T(8,128)}, u32[]{:S(2)}, u32[]{:S(2)}) async-start(f32[32,256,256]{2,0,1:T(8,128)} %copy.74), calls=%async_computation | async-start | bytes 16777216 | tf_op jit(solution)/shard_map/all_to_all | solution.py:51
  290.0 17.8 %copy-start.8 = (f32[256]{0:T(256)S(1)}, f32[256]{0:T(256)}, u32[]{:S(2)}) copy-start(f32[256]{0:T(256)} %param.26) | copy-start | bytes 3076
  316.5 23.6 %copy-start.4 = (f32[256,256]{1,0:T(8,128)S(1)}, f32[256,256]{1,0:T(8,128)}, u32[]{:S(2)}) copy-start(f32[256,256]{1,0:T(8,128)} %param.27) | copy-start | bytes 786436
  333.6 1.8 collective-permute-start.1
  336.7 10.1 %all-to-all-start.2 = ((f32[8,1,1024]{2,1,0:T(1,128)}), f32[8,1,1024]{2,1,0:T(1,128)S(1)}, u32[]{:S(2)}, u32[]{:S(2)}) async-start(f32[8,1,1024]{2,1,0:T(1,128)} %reshape.175), calls=%async_computation.2 | async-start | bytes 65536 | tf_op jit(solution)/shard_map/all_to_all | solution.py:64
  349.4 10.0 %all-to-all-start.3 = ((f32[8,1,1024]{2,1,0:T(1,128)}), f32[8,1,1024]{2,1,0:T(1,128)S(1)}, u32[]{:S(2)}, u32[]{:S(2)}) async-start(f32[8,1,1024]{2,1,0:T(1,128)} %reshape.177), calls=%async_computation.3 | async-start | bytes 65536 | tf_op jit(solution)/shard_map/all_to_all | solution.py:67
  402.3 3.3 collective-permute-start.2
  661.1 3.4 copy-start.1
  680.7 1.7 collective-permute-start.3
  694.6 13.7 %all-to-all-start.8 = ((f32[8,1,1024]{2,1,0:T(1,128)}), f32[8,1,1024]{2,1,0:T(1,128)S(1)}, u32[]{:S(2)}, u32[]{:S(2)}) async-start(f32[8,1,1024]{2,1,0:T(1,128)} %reshape.183), calls=%async_computation.8 | async-start | bytes 65536 | tf_op jit(solution)/shard_map/all_to_all | solution.py:67
  708.3 210.7 %all-to-all-start.5 = ((f32[256,32,256]{2,1,0:T(8,128)}), f32[256,32,256]{2,1,0:T(8,128)}, u32[]{:S(2)}, u32[]{:S(2)}) async-start(f32[256,32,256]{2,1,0:T(8,128)} %copy.92), calls=%async_computation.5 | async-start | bytes 16777216 | tf_op jit(solution)/shard_map/all_to_all | solution.py:19
where the time goes:
time: 959 us; the launch traced here: 954 us
  blocking collectives  455 us (47%)
  waiting for transfers between devices  202 us (21%)
  matrix products  143 us (15%)
  local copies, waits for them, and re-layouts  101 us (11%)
  starting transfers between devices  23.8 us (2%)
  other arithmetic  23.3 us (2%)
    psum x2, blocking collectives, on_device(): lax.psum((jnp.sum(jump * search), jnp.sum(search * search)), ('sub', 'sla...  239 us
    all_to_all x1, blocking collectives, on_device(): lax.all_to_all(part, 'slab', split_axis=1, concat_axis=0, tiled=True)  188 us
    all_to_all x1, waiting for transfers between devices, on_device(): lax.all_to_all(part, 'slab', split_axis=1, concat_axis=0, tiled=True)  184 us
    unnamed x34, local copies, waits for them, and re-layouts  38 us
    dot_general x2, matrix products, on_device(): modes = jnp.einsum('xjk,xi->ijk', lines, basis_x, precision=HI) / denom  35.5 us
    dot_general x2, matrix products, on_device(): part = jnp.einsum('xyz,zk->xyk', load, basis_z, precision=HI)  29.8 us
    transpose x2, local copies, waits for them, and re-layouts, on_device(): part = jnp.einsum('xyk,yj->xjk', part, basis_y, precision=HI)  20.6 us
    all_to_all x2, blocking collectives, on_device(): lax.all_to_all(edges, 'slab', split_axis=1, concat_axis=2, tiled=True)  20.2 us
  transfers between devices with their start and end apart: 9, of which 6 were waited for; matrix products, arithmetic and copies ran while one was open for 7% of the time, Pallas kernels for 0%

commit v1 on v0

v1 whole, which is shorter than its diff:
```python
import functools

import jax
import jax.numpy as jnp
from jax import lax
from jax.experimental import pallas as pl
from jax.experimental.pallas import tpu as pltpu
from jax.sharding import PartitionSpec as P

ITERS = 2
CHUNKS = 4

HI = lax.Precision.HIGHEST
MID = lax.Precision.HIGH
F32 = jnp.float32
BF16 = jnp.bfloat16


def split(value):
    top = value.astype(BF16)
    return top, (value - top.astype(F32)).astype(BF16)


def edge_kernel(part_ref, basis_ref, pair_ref, eigen_ref, first_ref, last_ref, out_ref):
    top, low = split(basis_ref[...])
    right = jnp.concatenate([top, low, top], axis=0)
    for at in range(part_ref.shape[0]):
        top, low = split(part_ref[at])
        left = jnp.concatenate([top, top, low], axis=0)
        hat = lax.dot_general(left, right, (((0,), (0,)), ((), ())), preferred_element_type=F32)
        modes = hat / (pair_ref[at : at + 1, :] + eigen_ref[...])
        out_ref[at, 0:1, :] = jnp.sum(modes * first_ref[...], axis=0, keepdims=True)
        out_ref[at, 1:2, :] = jnp.sum(modes * last_ref[...], axis=0, keepdims=True)


def partial_edges(part, basis_rows, pair, eigen, first, last):
    width, rows, depth = part.shape
    block = 8
    whole = lambda j: (0, 0)
    return pl.pallas_call(
        edge_kernel,
        out_shape=jax.ShapeDtypeStruct((width, 2, width), F32),
        grid=(width // block,),
        in_specs=[
            pl.BlockSpec((block, rows, depth), lambda j: (j, 0, 0)),
            pl.BlockSpec((rows, width), whole),
            pl.BlockSpec((block, width), lambda j: (j, 0)),
            pl.BlockSpec((depth, width), whole),
            pl.BlockSpec((depth, width), whole),
            pl.BlockSpec((depth, width), whole),
        ],
        out_specs=pl.BlockSpec((block, 2, width), lambda j: (j, 0, 0)),
        compiler_params=pltpu.CompilerParams(vmem_limit_bytes=24 * 2**20),
        cost_estimate=pl.CostEstimate(
            flops=2 * width * width * depth * 96, bytes_accessed=4 * width * rows * depth, transcendentals=0
        ),
        name="partial_edges",
    )(part, basis_rows, pair, eigen, first, last)


def face_step(edges, rho, basis_x, basis_y, face_stiff):
    apart = edges[:, :, 1] - jnp.roll(edges[:, :, 0], -1, axis=0)
    jump = jnp.einsum("sji,yj->syi", apart, basis_y, precision=HI)
    jump = jnp.einsum("syi,xi->sxy", jump, basis_x, precision=HI)
    face = jnp.einsum("sxy,yj->sxj", jump, basis_y, precision=HI)
    face = jnp.einsum("sxj,xi->sij", face, basis_x, precision=HI) * face_stiff
    face = jnp.einsum("sij,xi->sxj", face, basis_x, precision=HI)
    face = jnp.einsum("sxj,yj->sxy", face, basis_y, precision=HI)
    weights = 0.5 * (rho + jnp.roll(rho, -1))
    search = weights[:, None, None] * face
    alpha = jnp.sum(jump * search) / (jnp.sum(search * search) + 1e-06)
    return jump, search, alpha


def on_device(
    source, coarse, rho, basis_x, basis_y, basis_z, eigen_x, eigen_y, eigen_z, face_stiff
):
    field = source[0]
    rows, width = field.shape[:2]
    sub_index = lax.axis_index("sub")
    slab_index = lax.axis_index("slab")
    subs = lax.axis_size("sub")
    slabs = lax.axis_size("slab")
    own_rho = lax.dynamic_slice_in_dim(rho, sub_index, 1, 0)[0]
    piece = width // CHUNKS
    lot = piece // slabs
    edge_basis = jnp.stack([basis_z[0], basis_z[width - 1]])

    part = jnp.einsum("xyz,zk->xyk", field + coarse[1, 0], basis_z, precision=MID)
    lines = []
    for c in range(CHUNKS):
        some = jnp.einsum("xyk,yj->xjk", part, basis_y[:, c * piece : (c + 1) * piece], precision=MID)
        lines.append(lax.all_to_all(some, "slab", split_axis=1, concat_axis=0, tiled=True))

    early = jnp.einsum("xyz,zk->xyk", field + coarse[0, 0], basis_z, precision=MID)
    early = jnp.einsum("xyk,yj->jxk", early, basis_y, precision=MID)
    spread_out = lambda column: jnp.broadcast_to(column[:, None], (width, width))
    share = partial_edges(
        early,
        lax.dynamic_slice_in_dim(basis_x, slab_index * rows, rows, 0),
        eigen_y[:, None] + eigen_x[None, :],
        spread_out(eigen_z),
        spread_out(basis_z[0]),
        spread_out(basis_z[width - 1]),
    )
    edges = lax.psum_scatter(share, "slab", scatter_dimension=0, tiled=True) / own_rho
    edges = lax.all_gather(edges, ("sub", "slab"), axis=0, tiled=True)
    edges = edges.reshape(subs, width, 2, width)
    _, search, alpha = face_step(edges, rho, basis_x, basis_y, face_stiff)
    multipliers = alpha * search
    pair = jnp.stack([
        lax.dynamic_index_in_dim(multipliers, (sub_index + subs - 1) % subs, 0, keepdims=False),
        -lax.dynamic_index_in_dim(multipliers, sub_index, 0, keepdims=False),
    ])
    pair = jnp.einsum("pxy,yj->pxj", pair, basis_y, precision=HI)
    pair = jnp.einsum("pxj,xi->pij", pair, basis_x, precision=HI)

    fields = []
    edges = []
    for c in range(CHUNKS):
        start = c * piece + slab_index * lot
        eigen_part = lax.dynamic_slice_in_dim(eigen_y, start, lot, 0)
        pair_part = lax.dynamic_slice_in_dim(pair, start, lot, 2)
        denom = (eigen_x[:, None, None] + eigen_part[None, :, None] + eigen_z[None, None, :]) * own_rho
        hat = jnp.einsum("xjk,xi->ijk", lines[c], basis_x, precision=MID)
        hat = hat + pair_part[0][:, :, None] * edge_basis[0] + pair_part[1][:, :, None] * edge_basis[1]
        modes = hat / denom
        spread = jnp.einsum("ijk,xi->xjk", modes, basis_x, precision=MID)
        fields.append(lax.all_to_all(spread, "slab", split_axis=0, concat_axis=1, tiled=True))
        edges.append(jnp.einsum("ijk,pk->jpi", modes, edge_basis, precision=HI))

    edges = lax.all_gather(jnp.stack(edges), ("sub", "slab"), axis=0, tiled=False)
    edges = edges.reshape(subs, slabs, CHUNKS, lot, 2, width).swapaxes(1, 2).reshape(subs, width, 2, width)
    jump, search, alpha = face_step(edges, rho, basis_x, basis_y, face_stiff)
    multipliers = multipliers + alpha * search

    def own(face):
        face = lax.dynamic_index_in_dim(face, sub_index, 0, keepdims=True)
        return lax.dynamic_slice_in_dim(face, slab_index * rows, rows, 1)

    fields = [jnp.einsum("xjk,zk->xjz", some, basis_z, precision=MID) for some in fields]
    solution = jnp.einsum("xjz,yj->xyz", jnp.concatenate(fields, axis=1), basis_y, precision=MID)
    return (solution[None], own(multipliers), own(jump))


def solution(mesh):
    in_specs = (
        P("sub", "slab", None, None),
        P(None, "sub", "slab", None, None),
        P(),
        P(),
        P(),
        P(),
        P(),
        P(),
        P(),
        P(),
    )
    out_specs = (P("sub", "slab", None, None), P("sub", "slab", None), P("sub", "slab", None))
    return jax.shard_map(
        on_device, mesh=mesh, in_specs=in_specs, out_specs=out_specs, check_vma=False
    )
```

time: 959 us -> 620 us (0.65)
  blocking collectives: 455 us -> 0 us
  waiting for transfers between devices: 202 us -> 330 us
  matrix products: 143 us -> 113 us
  Pallas kernels: 0 us -> 24 us
  local copies, waits for them, and re-layouts: 101 us -> 82.9 us
  other arithmetic: 23.3 us -> 5.48 us
  starting transfers between devices: 23.8 us -> 38 us
  between operations: 5.17 us -> 17.9 us
    psum x2 -> x0, blocking collectives: 239 us -> none  [on_device(): lax.psum((jnp.sum(jump * search), jnp.sum(search * search)), ('sub', 'sla...]
    all_to_all x4 -> x0, blocking collectives: 217 us -> none  [the longest x1 188 us: on_device(): lax.all_to_all(part, 'slab', split_axis=1, concat_axis=0, tiled=True)]
    unnamed x0 -> x4, waiting for transfers between devices: none -> 72.3 us
    all_gather x0 -> x2, waiting for transfers between devices: none -> 52.7 us  [the longest x1 47.8 us: on_device(): edges = lax.all_gather(edges, ('sub', 'slab'), axis=0, tiled=True)]
    dot_general x20 -> x38, matrix products: 142 us -> 113 us  [the longest x4 20.8 us: on_device(): jnp.einsum('xyk,yj->xjk', part, basis_y[:, c * piece:(c + 1) * piece], pr...]
    pallas_call x0 -> x1, Pallas kernels: none -> 24 us  [partial_edges(): pl.pallas_call(edge_kernel, out_shape=jax.ShapeDtypeStruct((width, 2, wid...]
    all_to_all x5 -> x8, starting transfers between devices: 22.9 us -> 37.2 us  [the longest x4 20.3 us: on_device(): lax.all_to_all(some, 'slab', split_axis=1, concat_axis=0, tiled=True)]
    add x1 -> x2, other arithmetic: 13.9 us -> 1.18 us  [the longest x1 1.08 us: on_device(): multipliers = multipliers + alpha * search]
  transfers between devices with their start and end apart: 9 -> 11, of which waited for: 6 -> 9; matrix products, arithmetic and copies ran while one was open for 7% -> 27% of each run, Pallas kernels for 0% -> 4%
where the time goes in v1:
time: 620 us; the launch traced here: 611 us
  waiting for transfers between devices  330 us (53%)
  matrix products  113 us (18%)
  local copies, waits for them, and re-layouts  82.9 us (13%)
  starting transfers between devices  38 us (6%)
  Pallas kernels  24 us (4%)
  between operations  17.9 us (3%)
    all_to_all x4, waiting for transfers between devices, on_device(): lax.all_to_all(spread, 'slab', split_axis=0, concat_axis=1, tiled=True)  142 us
    unnamed x4, waiting for transfers between devices  72.3 us
    all_to_all x4, waiting for transfers between devices, on_device(): lax.all_to_all(some, 'slab', split_axis=1, concat_axis=0, tiled=True)  62.6 us
    all_gather x1, waiting for transfers between devices, on_device(): edges = lax.all_gather(edges, ('sub', 'slab'), axis=0, tiled=True)  47.8 us
    unnamed x57, local copies, waits for them, and re-layouts  29.4 us
    pallas_call x1, Pallas kernels, partial_edges(): pl.pallas_call(edge_kernel, out_shape=jax.ShapeDtypeStruct((width, 2, wid...  24 us
    dot_general x4, matrix products, on_device(): jnp.einsum('xyk,yj->xjk', part, basis_y[:, c * piece:(c + 1) * piece], pr...  20.8 us
    all_to_all x4, starting transfers between devices, on_device(): lax.all_to_all(some, 'slab', split_axis=1, concat_axis=0, tiled=True)  20.3 us
  transfers between devices with their start and end apart: 11, of which 9 were waited for; matrix products, arithmetic and copies ran while one was open for 27% of the time, Pallas kernels for 4%

profile of v1, /device:TPU:0, one launch (start us, length us, event | category | flops | bytes accessed | tf_op | source)
XLA Modules:
  0.0 611.1 jit_solution(17641877978844514982)
XLA Ops:
  7.2 7.9 %fusion.9 = f32[32,256,256]{2,1,0:T(8,128)S(1)} fusion(f32[1,32,256,256]{3,2,1,0:T(8,128)} %param.10, f32[2,1,32,256,256]{4,3,2,1,0:T(8,128)} %param.11, f32[256,256]{1,0:T(8,128)} %param.15), kind=kOutput, calls=%fused_computation.11 | convolution fusion | flops 3223322624 | bytes 25427968 | tf_op jit(solution)/shard_map/xyz,zk->xyk/dot_general | solution.py:89
  15.1 2.7 convolution_bitcast_fusion.3
  21.0 7.3 %all-to-all-start = ((f32[32,64,256]{2,0,1:T(8,128)}), f32[32,64,256]{2,0,1:T(8,128)S(1)}, u32[]{:S(2)}, u32[]{:S(2)}) async-start(f32[32,64,256]{2,0,1:T(8,128)} %copy.121), calls=%async_computation | async-start | bytes 4194304 | tf_op jit(solution)/shard_map/all_to_all | solution.py:93
  28.3 6.1 convolution_bitcast_fusion.2
  37.0 39.6 %all-to-all-done = f32[32,64,256]{2,0,1:T(8,128)S(1)} async-done(((f32[32,64,256]{2,0,1:T(8,128)}), f32[32,64,256]{2,0,1:T(8,128)S(1)}, u32[]{:S(2)}, u32[]{:S(2)}) %all-to-all-start) | async-done | bytes 2097184 | tf_op jit(solution)/shard_map/all_to_all | solution.py:93
  77.9 3.6 all-to-all-start.2
  82.1 7.9 %fusion.8 = f32[32,256,256]{1,2,0:T(8,128)S(1)} fusion(f32[1,32,256,256]{3,2,1,0:T(8,128)} %param.10, f32[2,1,32,256,256]{4,3,2,1,0:T(8,128)} %param.11, f32[256,256]{1,0:T(8,128)S(1)} %copy-done.4), kind=kOutput, calls=%fused_computation.9 | convolution fusion | flops 3223322624 | bytes 25427968 | tf_op jit(solution)/shard_map/xyz,zk->xyk/dot_general | solution.py:95
  90.0 5.7 fusion.79
  95.6 10.3 %copy.126 = f32[32,256,256]{1,0,2:T(8,128)} copy(f32[32,256,256]{2,1,0:T(8,128)} %fusion.79) | data formatting | bytes 16777216 | tf_op jit(solution)/shard_map/xyk,yj->jxk/dot_general | solution.py:96
  106.4 3.4 copy-done.1
  109.8 24.0 %partial_edges.1 = f32[256,2,256]{2,1,0:T(2,128)} custom-call(f32[256,32,256]{2,1,0:T(8,128)S(1)} %bitcast.306, f32[32,256]{1,0:T(8,128)S(1)} %constant_dynamic-slice_fusion.1.basis_ref, f32[256,256]{1,0:T(8,128)S(1)} %broadcast_add_fusion.pair_ref, f32[256,256]{1,0:T(8,128)S(1)} %broadcast_in_dim.12.eigen_ref, f32[256,256]{1,0:T(8,128)S(1)} %broadcast_in_dim.14.first_ref, ...), custom_call_target="tpu_custom_call" | custom-call | flops 3221225472 | bytes 8388608 | tf_op jit(solution)/shard_map/partial_edges/pallas_call | solution.py:40
  135.7 72.3 %all-reduce.3.cloned.1.call-done = f32[256,2,256]{2,1,0:T(2,128)} async-done(((f32[256,2,256]{2,1,0:T(2,128)}), f32[256,2,256]{2,1,0:T(2,128)}) %all-reduce.3.cloned.1.call-update) | async-done | bytes 524304
  210.1 6.0 convolution_bitcast_fusion.1
  218.7 4.7 all-to-all-start.4
  223.5 6.1 convolution_bitcast_fusion
  233.0 4.2 copy.123
  237.2 47.8 %all-gather.4.cloned.1.call-done = f32[1024,2,256]{2,1,0:T(2,128)} async-done(((f32[32,2,256]{2,1,0:T(2,128)}), f32[1024,2,256]{2,1,0:T(2,128)}) %all-gather.4.cloned.1.call-update) | async-done | bytes 2097168 | tf_op jit(solution)/shard_map/all_gather | solution.py:107
  285.0 3.8 slice.126
  290.4 3.6 copy.204
  294.0 3.0 copy.205
  297.9 4.7 all-to-all-start.6
  310.1 2.8 multiply_reduce_fusion.1
  317.5 3.5 fusion.32
  322.4 2.8 convolution_bitcast_fusion.7
  325.2 3.1 copy.138
  328.3 23.0 %all-to-all-done.6 = f32[32,64,256]{2,0,1:T(8,128)} async-done(((f32[32,64,256]{2,0,1:T(8,128)}), f32[32,64,256]{2,0,1:T(8,128)}, u32[]{:S(2)}, u32[]{:S(2)}) %all-to-all-start.6) | async-done | bytes 2097184 | tf_op jit(solution)/shard_map/all_to_all | solution.py:93
  351.3 4.4 all-to-all-start.1
  356.9 3.5 fusion.28
  364.7 39.0 %all-to-all-done.1 = f32[256,8,256]{2,1,0:T(8,128)} async-done(((f32[256,8,256]{2,1,0:T(8,128)}), f32[256,8,256]{2,1,0:T(8,128)}, u32[]{:S(2)}, u32[]{:S(2)}) %all-to-all-start.1) | async-done | bytes 2097184 | tf_op jit(solution)/shard_map/all_to_all | solution.py:129
  403.7 3.6 all-to-all-start.3
  407.3 2.8 copy.150
  410.1 3.5 fusion.24
  417.3 3.0 copy.152
  420.4 35.4 %all-to-all-done.3 = f32[256,8,256]{2,1,0:T(8,128)S(1)} async-done(((f32[256,8,256]{2,1,0:T(8,128)}), f32[256,8,256]{2,1,0:T(8,128)S(1)}, u32[]{:S(2)}, u32[]{:S(2)}) %all-to-all-start.3) | async-done | bytes 2097184 | tf_op jit(solution)/shard_map/all_to_all | solution.py:129
  455.7 4.5 all-to-all-start.5
  460.3 2.8 copy.157
  463.1 3.5 fusion.20
  470.2 3.0 copy.159
  473.2 2.8 convolution_bitcast_fusion.18
  477.2 30.9 %all-to-all-done.5 = f32[256,8,256]{2,1,0:T(8,128)} async-done(((f32[256,8,256]{2,1,0:T(8,128)}), f32[256,8,256]{2,1,0:T(8,128)}, u32[]{:S(2)}, u32[]{:S(2)}) %all-to-all-start.5) | async-done | bytes 2097184 | tf_op jit(solution)/shard_map/all_to_all | solution.py:129
  508.1 4.4 all-to-all-start.7
  512.7 2.8 convolution_bitcast_fusion.16
  517.4 4.0 fusion.29
  526.3 36.8 %all-to-all-done.7 = f32[256,8,256]{2,1,0:T(8,128)} async-done(((f32[256,8,256]{2,1,0:T(8,128)}), f32[256,8,256]{2,1,0:T(8,128)}, u32[]{:S(2)}, u32[]{:S(2)}) %all-to-all-start.7) | async-done | bytes 2097184 | tf_op jit(solution)/shard_map/all_to_all | solution.py:129
  563.1 2.8 fusion.17
  566.0 9.5 %fusion.14 = f32[1,32,256,256]{2,3,1,0:T(8,128)} fusion(f32[32,64,256]{2,1,0:T(8,128)S(1)} %fusion.17, f32[32,64,256]{2,1,0:T(8,128)S(1)} %fusion.21, f32[32,64,256]{2,1,0:T(8,128)S(1)} %copy-done.13, f32[32,64,256]{2,1,0:T(8,128)S(1)} %copy-done.12, f32[256,256]{1,0:T(8,128)S(1)} %copy-done.3), kind=kOutput, calls=%fused_computation.16 | convolution fusion | flops 3227516928 | bytes 17039360 | tf_op jit(solution)/shard_map/xjz,yj->xyz/dot_general | solution.py:142
  575.5 9.0 %copy.176 = f32[1,32,256,256]{3,2,1,0:T(8,128)} copy(f32[1,32,256,256]{2,3,1,0:T(8,128)} %fusion.14) | data formatting | bytes 16777216
  584.5 4.9 all-gather.6.cloned.1.call-done
  (116 shorter events, 66.7 us)
Async XLA Ops:
  7.2 98.8 %copy-start = (f32[256,256]{1,0:T(8,128)S(1)}, f32[256,256]{1,0:T(8,128)}, u32[]{:S(2)}) copy-start(f32[256,256]{1,0:T(8,128)} %param.13) | copy-start | bytes 786436
  7.2 7.9 %copy-start.3 = (f32[256,256]{1,0:T(8,128)S(1)}, f32[256,256]{1,0:T(8,128)}, u32[]{:S(2)}) copy-start(f32[256,256]{1,0:T(8,128)} %param.14) | copy-start | bytes 786436
  15.1 3.4 copy-start.2
  21.0 55.5 %all-to-all-start = ((f32[32,64,256]{2,0,1:T(8,128)}), f32[32,64,256]{2,0,1:T(8,128)S(1)}, u32[]{:S(2)}, u32[]{:S(2)}) async-start(f32[32,64,256]{2,0,1:T(8,128)} %copy.121), calls=%async_computation | async-start | bytes 4194304 | tf_op jit(solution)/shard_map/all_to_all | solution.py:93
  37.0 45.1 %copy-start.4 = (f32[256,256]{1,0:T(8,128)S(1)}, f32[256,256]{1,0:T(8,128)}, u32[]{:S(2)}) copy-start(f32[256,256]{1,0:T(8,128)} %param.15) | copy-start | bytes 786436
  76.6 1.3 copy-start.5
  77.9 140.7 %all-to-all-start.2 = ((f32[32,64,256]{2,0,1:T(8,128)}), f32[32,64,256]{2,0,1:T(8,128)S(1)}, u32[]{:S(2)}, u32[]{:S(2)}) async-start(f32[32,64,256]{2,0,1:T(8,128)} %copy.141), calls=%async_computation.2 | async-start | bytes 4194304 | tf_op jit(solution)/shard_map/all_to_all | solution.py:93
  81.6 126.4 %all-reduce.3.cloned.1.call-start = ((), (), s32[]{:S(2)}) async-start(), calls=%async_computation.10 | async-start | bytes 1048576
  95.6 10.3 %copy-start.20 = (f32[256]{0:T(256)S(1)}, f32[256]{0:T(256)}, u32[]{:S(2)}) copy-start(f32[256]{0:T(256)} %param.17) | copy-start | bytes 3076
  95.6 10.4 %copy-start.22 = (f32[256]{0:T(256)S(1)}, f32[256]{0:T(256)}, u32[]{:S(2)}) copy-start(f32[256]{0:T(256)} %param.16) | copy-start | bytes 3076
  95.6 10.7 %copy-start.23 = (f32[256]{0:T(256)S(1)}, f32[256]{0:T(256)}, u32[]{:S(2)}) copy-start(f32[256]{0:T(256)} %param.18) | copy-start | bytes 3076
  106.4 3.4 copy-start.1
  109.8 24.0 %copy-start.24 = (u32[32]{0:T(128)S(1)}, u32[32]{0:T(128)}, u32[]{:S(2)}) copy-start(u32[32]{0:T(128)} %constant.96) | copy-start | bytes 388
  109.8 25.3 %copy-start.21 = (f32[4]{0:T(128)S(1)}, f32[4]{0:T(128)}, u32[]{:S(2)}) copy-start(f32[4]{0:T(128)} %param.12) | copy-start | bytes 52
  133.8 151.2 %all-gather.4.cloned.1.call-start = ((), (), s32[]{:S(2)}) async-start(), calls=%async_computation.8 | async-start | bytes 2162688 | tf_op jit(solution)/shard_map/all_gather | solution.py:107
  218.7 4.8 copy-start.19
  218.7 79.2 %all-to-all-start.4 = ((f32[32,64,256]{2,0,1:T(8,128)}), f32[32,64,256]{2,0,1:T(8,128)}, u32[]{:S(2)}, u32[]{:S(2)}) async-start(f32[32,64,256]{2,0,1:T(8,128)} %copy.148), calls=%async_computation.4 | async-start | bytes 4194304 | tf_op jit(solution)/shard_map/all_to_all | solution.py:93
  285.0 3.8 copy-start.16
  297.9 4.7 copy-start.18
  297.9 53.4 %all-to-all-start.6 = ((f32[32,64,256]{2,0,1:T(8,128)}), f32[32,64,256]{2,0,1:T(8,128)}, u32[]{:S(2)}, u32[]{:S(2)}) async-start(f32[32,64,256]{2,0,1:T(8,128)} %copy.155), calls=%async_computation.6 | async-start | bytes 4194304 | tf_op jit(solution)/shard_map/all_to_all | solution.py:93
  315.5 1.4 copy-start.15
  315.6 2.0 copy-start.17
  321.0 1.4 copy-start.6
  351.3 52.4 %all-to-all-start.1 = ((f32[256,8,256]{2,1,0:T(8,128)}), f32[256,8,256]{2,1,0:T(8,128)}, u32[]{:S(2)}, u32[]{:S(2)}) async-start(f32[256,8,256]{2,1,0:T(8,128)} %copy.138), calls=%async_computation.1 | async-start | bytes 4194304 | tf_op jit(solution)/shard_map/all_to_all | solution.py:129
  360.4 1.3 copy-start.7
  403.7 52.0 %all-to-all-start.3 = ((f32[256,8,256]{2,1,0:T(8,128)}), f32[256,8,256]{2,1,0:T(8,128)S(1)}, u32[]{:S(2)}, u32[]{:S(2)}) async-start(f32[256,8,256]{2,1,0:T(8,128)} %copy.145), calls=%async_computation.3 | async-start | bytes 4194304 | tf_op jit(solution)/shard_map/all_to_all | solution.py:129
  413.6 1.4 copy-start.9
  455.7 52.3 %all-to-all-start.5 = ((f32[256,8,256]{2,1,0:T(8,128)}), f32[256,8,256]{2,1,0:T(8,128)}, u32[]{:S(2)}, u32[]{:S(2)}) async-start(f32[256,8,256]{2,1,0:T(8,128)} %copy.152), calls=%async_computation.5 | async-start | bytes 4194304 | tf_op jit(solution)/shard_map/all_to_all | solution.py:129
  466.6 1.3 copy-start.10
  473.2 2.8 copy-start.8
  508.1 55.0 %all-to-all-start.7 = ((f32[256,8,256]{2,1,0:T(8,128)}), f32[256,8,256]{2,1,0:T(8,128)}, u32[]{:S(2)}, u32[]{:S(2)}) async-start(f32[256,8,256]{2,1,0:T(8,128)} %copy.159), calls=%async_computation.7 | async-start | bytes 4194304 | tf_op jit(solution)/shard_map/all_to_all | solution.py:129
  512.5 76.9 %all-gather.6.cloned.1.call-start = ((), (), s32[]{:S(2)}) async-start(), calls=%async_computation.9 | async-start | bytes 2162688 | tf_op jit(solution)/shard_map/all_gather | solution.py:132
  512.7 2.8 copy-start.11
  563.1 2.8 copy-start.12
  563.1 2.9 copy-start.13
  596.7 2.0 copy-start.14
Sparse Core Ops, SparseCore 0:
  133.9 74.0 all-reduce.2
  211.0 73.9 all-gather.3
  517.5 71.8 all-gather.5

commit v2 on v1

v2 whole, which is shorter than its diff:
```python
import jax
import jax.numpy as jnp
from jax import lax
from jax.experimental import pallas as pl
from jax.experimental.pallas import tpu as pltpu
from jax.sharding import PartitionSpec as P

ITERS = 2
CHUNKS = 4

HI = lax.Precision.HIGHEST
MID = lax.Precision.HIGH
F32 = jnp.float32
BF16 = jnp.bfloat16


def split(value):
    top = value.astype(BF16)
    return top, (value - top.astype(F32)).astype(BF16)


def edge_kernel(part_ref, basis_ref, pair_ref, eigen_ref, first_ref, last_ref, out_ref):
    top, low = split(basis_ref[...])
    right = jnp.concatenate([top, low, top], axis=0)
    for at in range(part_ref.shape[0]):
        top, low = split(part_ref[at])
        left = jnp.concatenate([top, top, low], axis=0)
        hat = lax.dot_general(left, right, (((0,), (0,)), ((), ())), preferred_element_type=F32)
        modes = hat / (pair_ref[at : at + 1, :] + eigen_ref[...])
        width = basis_ref.shape[1]
        out_ref[at : at + 1, :width] = jnp.sum(modes * first_ref[...], axis=0, keepdims=True)
        out_ref[at : at + 1, width:] = jnp.sum(modes * last_ref[...], axis=0, keepdims=True)


def partial_edges(part, basis_rows, pair, eigen, first, last):
    width, rows, depth = part.shape
    block = 8
    whole = lambda j: (0, 0)
    return pl.pallas_call(
        edge_kernel,
        out_shape=jax.ShapeDtypeStruct((width, 2 * width), F32),
        grid=(width // block,),
        in_specs=[
            pl.BlockSpec((block, rows, depth), lambda j: (j, 0, 0)),
            pl.BlockSpec((rows, width), whole),
            pl.BlockSpec((block, width), lambda j: (j, 0)),
            pl.BlockSpec((depth, width), whole),
            pl.BlockSpec((depth, width), whole),
            pl.BlockSpec((depth, width), whole),
        ],
        out_specs=pl.BlockSpec((block, 2 * width), lambda j: (j, 0)),
        compiler_params=pltpu.CompilerParams(vmem_limit_bytes=24 * 2**20),
        cost_estimate=pl.CostEstimate(
            flops=2 * width * width * depth * 96, bytes_accessed=4 * width * rows * depth, transcendentals=0
        ),
        name="partial_edges",
    )(part, basis_rows, pair, eigen, first, last)


def last_kernel(*refs):
    basis_ref, out_ref = refs[-2:]
    top, low = split(basis_ref[...])
    left = jnp.concatenate([top, top, low], axis=1)
    for at in range(out_ref.shape[0]):
        top, low = split(jnp.concatenate([ref[at] for ref in refs[:-2]], axis=0))
        right = jnp.concatenate([top, low, top], axis=0)
        out_ref[at] = jnp.dot(left, right, preferred_element_type=F32)


def last_product(fields, basis_y):
    rows, piece, depth = fields[0].shape
    width = basis_y.shape[0]
    block = 4
    return pl.pallas_call(
        last_kernel,
        out_shape=jax.ShapeDtypeStruct((rows, width, depth), F32),
        grid=(rows // block,),
        in_specs=[pl.BlockSpec((block, piece, depth), lambda x: (x, 0, 0))] * len(fields)
        + [pl.BlockSpec((width, width), lambda x: (0, 0))],
        out_specs=pl.BlockSpec((block, width, depth), lambda x: (x, 0, 0)),
        compiler_params=pltpu.CompilerParams(vmem_limit_bytes=24 * 2**20),
        name="last_product",
    )(*fields, basis_y)


def from_behind(block, axis, distance):
    count = lax.axis_size(axis)
    return lax.ppermute(block, axis, [((i - distance) % count, i) for i in range(count)])


def exchange(blocks, extra, before):
    size = blocks.shape[1]
    if extra is not None:
        blocks = jnp.concatenate([blocks, extra], axis=1)
    if before:
        blocks, _ = lax.optimization_barrier((blocks, before[-1]))
    got = lax.all_to_all(blocks, "slab", split_axis=0, concat_axis=0, tiled=True)
    before.append(got)
    return got[:, :size], got[:, size:]


def face_step(apart, weight, basis_x, basis_y, face_stiff):
    subs = lax.axis_size("sub")
    jump = jnp.einsum("ji,yj->yi", apart, basis_y, precision=HI)
    jump = jnp.einsum("yi,xi->xy", jump, basis_x, precision=HI)
    face = jnp.einsum("xy,yj->xj", jump, basis_y, precision=HI)
    face = jnp.einsum("xj,xi->ij", face, basis_x, precision=HI) * face_stiff
    face = jnp.einsum("ij,xi->xj", face, basis_x, precision=HI)
    face = jnp.einsum("xj,yj->xy", face, basis_y, precision=HI)
    search = weight * face
    sums = jnp.stack([jnp.sum(jump * search), jnp.sum(search * search)])
    sums = jnp.broadcast_to(sums[:, None], (2, 128))
    total = sums
    for distance in range(1, subs):
        total = total + from_behind(sums, "sub", distance)
    return jump, search, total[0, 0] / (total[1, 0] + 1e-06)


def on_device(
    source, coarse, rho, basis_x, basis_y, basis_z, eigen_x, eigen_y, eigen_z, face_stiff
):
    field = source[0]
    rows, width = field.shape[:2]
    sub_index = lax.axis_index("sub")
    slab_index = lax.axis_index("slab")
    subs = lax.axis_size("sub")
    slabs = lax.axis_size("slab")
    own_rho = lax.dynamic_slice_in_dim(rho, sub_index, 1, 0)[0]
    next_rho = lax.dynamic_slice_in_dim(rho, (sub_index + 1) % subs, 1, 0)[0]
    weight = 0.5 * (own_rho + next_rho)
    piece = width // CHUNKS
    lot = piece // slabs
    edge_basis = jnp.stack([basis_z[0], basis_z[width - 1]])
    before = []

    part = jnp.einsum("xyz,zk->xyk", field + coarse[1, 0], basis_z, precision=MID)

    def outward(c, extra=None):
        some = jnp.einsum("xyk,yj->xjk", part, basis_y[:, c * piece : (c + 1) * piece], precision=MID)
        some = some.reshape(rows, slabs, lot, width).swapaxes(0, 1)
        some, extra = exchange(some, extra, before)
        return some.reshape(width, lot, width), extra

    lines = [outward(0)[0]]

    early = jnp.einsum("xyz,zk->xyk", field + coarse[0, 0], basis_z, precision=MID)
    early = jnp.einsum("xyk,yj->jxk", early, basis_y, precision=MID)
    spread_out = lambda column: jnp.broadcast_to(column[:, None], (width, width))
    share = partial_edges(
        early,
        lax.dynamic_slice_in_dim(basis_x, slab_index * rows, rows, 0),
        eigen_y[:, None] + eigen_x[None, :],
        spread_out(eigen_z),
        spread_out(basis_z[0]),
        spread_out(basis_z[width - 1]),
    )
    some, extra = outward(1, share.reshape(slabs, 2 * CHUNKS, lot, width))
    lines.append(some)
    edges = jnp.sum(extra, axis=0).reshape(width // slabs, 2 * width) / own_rho
    apart = edges[:, width:] - from_behind(edges[:, :width], "sub", -1)
    apart = jnp.broadcast_to(apart.reshape(1, CHUNKS, lot, width), (slabs, CHUNKS, lot, width))
    some, extra = outward(2, apart)
    lines.append(some)
    lines.append(outward(3)[0])
    _, search, alpha = face_step(extra.reshape(width, width), weight, basis_x, basis_y, face_stiff)
    multipliers = alpha * search
    pair = jnp.stack([alpha * from_behind(search, "sub", 1), -multipliers])
    pair = jnp.einsum("pxy,yj->pxj", pair, basis_y, precision=HI)
    pair = jnp.einsum("pxj,xi->pij", pair, basis_x, precision=HI)

    def modal(c):
        start = c * piece + slab_index * lot
        eigen_part = lax.dynamic_slice_in_dim(eigen_y, start, lot, 0)
        pair_part = lax.dynamic_slice_in_dim(pair, start, lot, 2)
        denom = (eigen_x[:, None, None] + eigen_part[None, :, None] + eigen_z[None, None, :]) * own_rho
        hat = jnp.einsum("xjk,xi->ijk", lines[c], basis_x, precision=MID)
        hat = hat + pair_part[0][:, :, None] * edge_basis[0] + pair_part[1][:, :, None] * edge_basis[1]
        modes = hat / denom
        spread = jnp.einsum("ijk,xi->xjk", modes, basis_x, precision=MID)
        edges = jnp.einsum("ijk,pk->pji", modes, edge_basis, precision=HI)
        return spread.reshape(slabs, rows, lot, width), edges

    def inward(spread, extra=None):
        some, extra = exchange(spread, extra, before)
        some = jnp.einsum("dxjk,zk->xdjz", some, basis_z, precision=MID)
        return some.reshape(rows, piece, width), extra

    spreads, edges = zip(*[modal(c) for c in range(CHUNKS)])
    edges = jnp.stack(edges, axis=1)
    apart = edges[1] - from_behind(edges[0], "sub", -1)
    apart = jnp.broadcast_to(apart[None], (slabs, CHUNKS, lot, width))
    fields = [inward(spreads[0])[0], inward(spreads[1])[0]]
    some, extra = inward(spreads[2], apart)
    fields.append(some)
    extra = extra.swapaxes(0, 1).reshape(width, width)
    jump, search, alpha = face_step(extra, weight, basis_x, basis_y, face_stiff)
    multipliers = multipliers + alpha * search
    own = lambda face: lax.dynamic_slice_in_dim(face, slab_index * rows, rows, 0)
    fields.append(inward(spreads[3])[0])
    solution = last_product(fields, basis_y)
    return (solution[None], own(multipliers)[None], own(jump)[None])


def solution(mesh):
    in_specs = (
        P("sub", "slab", None, None),
        P(None, "sub", "slab", None, None),
        P(),
        P(),
        P(),
        P(),
        P(),
        P(),
        P(),
        P(),
    )
    out_specs = (P("sub", "slab", None, None), P("sub", "slab", None), P("sub", "slab", None))
    return jax.shard_map(
        on_device, mesh=mesh, in_specs=in_specs, out_specs=out_specs, check_vma=False
    )
```

time: 620 us -> 513 us (0.83)
  waiting for transfers between devices: 330 us -> 271 us
  local copies, waits for them, and re-layouts: 82.9 us -> 51.1 us
  matrix products: 113 us -> 92.9 us
  between operations: 17.9 us -> 5.55 us
  starting transfers between devices: 38 us -> 47.1 us
  Pallas kernels: 24 us -> 30.3 us
    unnamed x4 -> x0, waiting for transfers between devices: 72.3 us -> none
    all_to_all x8, waiting for transfers between devices: 205 us -> 268 us  [exchange(): lax.all_to_all(blocks, 'slab', split_axis=0, concat_axis=0, tiled=True)]
    all_gather x2 -> x0, waiting for transfers between devices: 52.7 us -> none  [the longest x1 47.8 us: on_device(): edges = lax.all_gather(edges, ('sub', 'slab'), axis=0, tiled=True)]
    dot_general x33 -> x32, matrix products: 90.5 us -> 70.2 us  [the longest x4 20.8 us: outward(): jnp.einsum('xyk,yj->xjk', part, basis_y[:, c * piece:(c + 1) * piece], pr...]
    unnamed x57 -> x47, local copies, waits for them, and re-layouts: 29.4 us -> 12.2 us
    optimization_barrier x0 -> x3, local copies, waits for them, and re-layouts: none -> 11.8 us  [exchange(): blocks, _ = lax.optimization_barrier((blocks, before[-1]))]
    dot_general x5 -> x1, local copies, waits for them, and re-layouts: 12.5 us -> 0.85 us  [face_step(): jump = jnp.einsum('yi,xi->xy', jump, basis_x, precision=HI)]
    all_to_all x4 -> x0, local copies, waits for them, and re-layouts: 10.9 us -> none  [on_device(): lax.all_to_all(some, 'slab', split_axis=1, concat_axis=0, tiled=True)]
  transfers between devices with their start and end apart: 11 -> 17, of which waited for: 9 -> 10; matrix products, arithmetic and copies ran while one was open for 27% -> 22% of each run, Pallas kernels for 4% -> 5%
where the time goes in v2:
time: 513 us; the launch traced here: 508 us
  waiting for transfers between devices  271 us (53%)
  matrix products  92.9 us (18%)
  local copies, waits for them, and re-layouts  51.1 us (10%)
  starting transfers between devices  47.1 us (9%)
  Pallas kernels  30.3 us (6%)
  other arithmetic  9.51 us (2%)
  between operations  5.55 us (1%)
    all_to_all x8, waiting for transfers between devices, exchange(): lax.all_to_all(blocks, 'slab', split_axis=0, concat_axis=0, tiled=True)  268 us
    all_to_all x8, starting transfers between devices, exchange(): lax.all_to_all(blocks, 'slab', split_axis=0, concat_axis=0, tiled=True)  39.2 us
    pallas_call x1, Pallas kernels, partial_edges(): pl.pallas_call(edge_kernel, out_shape=jax.ShapeDtypeStruct((width, 2 * wi...  23.4 us
    dot_general x4, matrix products, outward(): jnp.einsum('xyk,yj->xjk', part, basis_y[:, c * piece:(c + 1) * piece], pr...  20.8 us
    dot_general x4, matrix products, modal(): hat = jnp.einsum('xjk,xi->ijk', lines[c], basis_x, precision=MID)  17 us
    unnamed x47, local copies, waits for them, and re-layouts  12.2 us
    optimization_barrier x3, local copies, waits for them, and re-layouts, exchange(): blocks, _ = lax.optimization_barrier((blocks, before[-1]))  11.8 us
    dot_general x1, local copies, waits for them, and re-layouts, on_device(): early = jnp.einsum('xyk,yj->jxk', early, basis_y, precision=MID)  10.3 us
  transfers between devices with their start and end apart: 17, of which 10 were waited for; matrix products, arithmetic and copies ran while one was open for 22% of the time, Pallas kernels for 5%

profile of v2, /device:TPU:0, one launch (start us, length us, event | category | flops | bytes accessed | tf_op | source)
XLA Modules:
  0.0 507.8 jit_solution(17315754708456010203)
XLA Ops:
  0.7 7.9 %fusion.1 = f32[32,256,256]{2,1,0:T(8,128)S(1)} fusion(f32[1,32,256,256]{3,2,1,0:T(8,128)} %param.10, f32[2,1,32,256,256]{4,3,2,1,0:T(8,128)} %param.11, f32[256,256]{1,0:T(8,128)} %param.15), kind=kOutput, calls=%fused_computation.3 | convolution fusion | flops 3223322624 | bytes 25427968 | tf_op jit(solution)/shard_map/xyz,zk->xyk/dot_general | solution.py:136
  8.6 2.7 convolution_bitcast_fusion.3
  13.3 7.7 %all-to-all-start = ((f32[8,32,8,256]{3,2,1,0:T(8,128)}), f32[8,32,8,256]{3,2,1,0:T(8,128)}, u32[]{:S(2)}, u32[]{:S(2)}) async-start(f32[8,32,8,256]{3,2,1,0:T(8,128)} %bitcast.295), calls=%async_computation | async-start | bytes 4194304 | tf_op jit(solution)/shard_map/all_to_all | solution.py:97
  21.0 7.9 %fusion = f32[32,256,256]{1,2,0:T(8,128)S(1)} fusion(f32[1,32,256,256]{3,2,1,0:T(8,128)} %param.10, f32[2,1,32,256,256]{4,3,2,1,0:T(8,128)} %param.11, f32[256,256]{1,0:T(8,128)S(1)} %copy-done.8), kind=kOutput, calls=%fused_computation.1 | convolution fusion | flops 3223322624 | bytes 25427968 | tf_op jit(solution)/shard_map/xyz,zk->xyk/dot_general | solution.py:146
  28.9 5.7 %fusion.43 = f32[32,256,256]{2,1,0:T(8,128)} fusion(f32[32,256,256]{1,2,0:T(8,128)S(1)} %fusion, f32[256,256]{1,0:T(8,128)S(1)} %copy-done.1), kind=kOutput, calls=%fused_computation.72 | convolution fusion | flops 3221225472 | bytes 17039360 | tf_op jit(solution)/shard_map/xyk,yj->jxk/dot_general | solution.py:147
  34.6 10.3 %copy.50 = f32[32,256,256]{1,0,2:T(8,128)} copy(f32[32,256,256]{2,1,0:T(8,128)} %fusion.43) | data formatting | bytes 16777216 | tf_op jit(solution)/shard_map/xyk,yj->jxk/dot_general | solution.py:147
  45.4 3.4 copy-done.2
  48.8 23.4 %partial_edges.1 = f32[256,512]{1,0:T(8,128)S(1)} custom-call(f32[256,32,256]{2,1,0:T(8,128)S(1)} %bitcast.297, f32[32,256]{1,0:T(8,128)S(1)} %constant_dynamic-slice_fusion.basis_ref, f32[256,256]{1,0:T(8,128)S(1)} %broadcast_add_fusion.pair_ref, f32[256,256]{1,0:T(8,128)S(1)} %broadcast_in_dim.26.eigen_ref, f32[256,256]{1,0:T(8,128)S(1)} %broadcast_in_dim.28.first_ref, ...), custom_call_target="tpu_custom_call" | custom-call | flops 3221225472 | bytes 8388608 | tf_op jit(solution)/shard_map/partial_edges/pallas_call | solution.py:39
  72.3 6.1 %convolution_bitcast_fusion.1 = f32[32,8,8,256]{3,2,1,0:T(8,128)S(1)} fusion(f32[32,256,256]{2,1,0:T(8,128)} %copy-done.5, f32[256,256]{1,0:T(8,128)S(1)} %copy-done.1), kind=kOutput, calls=%fused_computation.40 | convolution fusion | flops 805306368 | bytes 10616832 | tf_op jit(solution)/shard_map/xyk,yj->xjk/dot_general | solution.py:139
  78.6 1.7 pad_maximum_fusion
  80.3 6.1 %all-to-all-start.1 = ((f32[8,40,8,256]{3,2,1,0:T(8,128)}), f32[8,40,8,256]{3,2,1,0:T(8,128)S(1)}, u32[]{:S(2)}, u32[]{:S(2)}) async-start(f32[8,40,8,256]{3,2,1,0:T(8,128)} %pad_maximum_fusion), calls=%async_computation.1 | async-start | bytes 5242880 | tf_op jit(solution)/shard_map/all_to_all | solution.py:97
  87.0 58.3 %all-to-all-done.1 = f32[8,40,8,256]{3,2,1,0:T(8,128)S(1)} async-done(((f32[8,40,8,256]{3,2,1,0:T(8,128)}), f32[8,40,8,256]{3,2,1,0:T(8,128)S(1)}, u32[]{:S(2)}, u32[]{:S(2)}) %all-to-all-start.1) | async-done | bytes 2621472 | tf_op jit(solution)/shard_map/all_to_all | solution.py:97
  146.1 5.9 %convolution_bitcast_fusion.2 = f32[32,8,8,256]{3,2,1,0:T(8,128)S(1)} fusion(f32[32,256,256]{2,1,0:T(8,128)} %copy-done.5, f32[256,256]{1,0:T(8,128)S(1)} %copy-done.1), kind=kOutput, calls=%fused_computation.41 | convolution fusion | flops 805306368 | bytes 10616832 | tf_op jit(solution)/shard_map/xyk,yj->xjk/dot_general | solution.py:139
  152.3 1.6 pad_maximum_fusion.1
  153.9 4.9 all-to-all-start.2
  160.1 6.1 %convolution_bitcast_fusion = f32[32,8,8,256]{3,2,1,0:T(8,128)S(1)} fusion(f32[32,256,256]{2,1,0:T(8,128)} %copy-done.5, f32[256,256]{1,0:T(8,128)S(1)} %copy-done.1), kind=kOutput, calls=%fused_computation.39 | convolution fusion | flops 805306368 | bytes 10616832 | tf_op jit(solution)/shard_map/xyk,yj->xjk/dot_general | solution.py:139
  167.8 45.5 %all-to-all-done.2 = f32[8,36,8,256]{3,2,1,0:T(8,128)} async-done(((f32[8,36,8,256]{3,2,1,0:T(8,128)}), f32[8,36,8,256]{3,2,1,0:T(8,128)}, u32[]{:S(2)}, u32[]{:S(2)}) %all-to-all-start.2) | async-done | bytes 2359328 | tf_op jit(solution)/shard_map/all_to_all | solution.py:97
  216.2 4.4 all-to-all-start.3
  220.6 1.6 fusion.80
  233.6 2.3 collective-permute-done.4
  237.3 5.0 fusion.13
  243.6 2.3 fusion.54
  246.0 22.5 %all-to-all-done.3 = f32[8,32,8,256]{3,2,1,0:T(8,128)} async-done(((f32[8,32,8,256]{3,2,1,0:T(8,128)}), f32[8,32,8,256]{3,2,1,0:T(8,128)}, u32[]{:S(2)}, u32[]{:S(2)}) %all-to-all-start.3) | async-done | bytes 2097184 | tf_op jit(solution)/shard_map/all_to_all | solution.py:97
  268.5 4.2 copy.55
  272.7 4.4 all-to-all-start.4
  277.2 3.5 fusion.11
  283.1 41.8 %all-to-all-done.4 = f32[8,32,8,256]{3,2,1,0:T(8,128)} async-done(((f32[8,32,8,256]{3,2,1,0:T(8,128)}), f32[8,32,8,256]{3,2,1,0:T(8,128)}, u32[]{:S(2)}, u32[]{:S(2)}) %all-to-all-start.4) | async-done | bytes 2097184 | tf_op jit(solution)/shard_map/all_to_all | solution.py:97
  324.9 2.6 copy.59
  327.5 3.8 all-to-all-start.5
  331.3 1.9 slice.131
  336.2 3.5 fusion.9
  340.7 5.0 fusion.7
  350.5 1.6 pad_maximum_fusion.2
  352.0 27.5 %all-to-all-done.5 = f32[8,32,8,256]{3,2,1,0:T(8,128)S(1)} async-done(((f32[8,32,8,256]{3,2,1,0:T(8,128)}), f32[8,32,8,256]{3,2,1,0:T(8,128)S(1)}, u32[]{:S(2)}, u32[]{:S(2)}) %all-to-all-start.5) | async-done | bytes 2097184 | tf_op jit(solution)/shard_map/all_to_all | solution.py:97
  380.9 3.6 all-to-all-start.6
  384.6 4.0 fusion.45
  388.5 50.1 %all-to-all-done.6 = f32[8,36,8,256]{3,2,1,0:T(8,128)S(1)} async-done(((f32[8,36,8,256]{3,2,1,0:T(8,128)}), f32[8,36,8,256]{3,2,1,0:T(8,128)S(1)}, u32[]{:S(2)}, u32[]{:S(2)}) %all-to-all-start.6) | async-done | bytes 2359328 | tf_op jit(solution)/shard_map/all_to_all | solution.py:97
  438.6 5.0 copy.72
  443.6 4.4 all-to-all-start.7
  448.0 2.6 convolution_bitcast_fusion.7
  453.2 1.6 copy.125
  458.1 1.7 fusion.30
  460.4 2.0 fusion.36
  463.8 1.7 collective-permute-start.7
  465.6 1.7 collective-permute-start.8
  473.2 22.5 %all-to-all-done.7 = f32[8,32,8,256]{3,2,1,0:T(8,128)} async-done(((f32[8,32,8,256]{3,2,1,0:T(8,128)}), f32[8,32,8,256]{3,2,1,0:T(8,128)}, u32[]{:S(2)}, u32[]{:S(2)}) %all-to-all-start.7) | async-done | bytes 2097184 | tf_op jit(solution)/shard_map/all_to_all | solution.py:97
  495.7 2.6 convolution_bitcast_fusion.5
  500.6 6.9 %last_product.1 = f32[32,256,256]{2,1,0:T(8,128)} custom-call(f32[32,64,256]{2,1,0:T(8,128)S(1)} %bitcast.298, f32[32,64,256]{2,1,0:T(8,128)S(1)} %bitcast.299, f32[32,64,256]{2,1,0:T(8,128)S(1)} %bitcast.300, f32[32,64,256]{2,1,0:T(8,128)S(1)} %bitcast.301, f32[256,256]{1,0:T(8,128)S(1)} %copy-done.1), custom_call_target="tpu_custom_call" | custom-call | tf_op jit(solution)/shard_map/last_product/pallas_call | solution.py:74
  (131 shorter events, 48.9 us)
Async XLA Ops:
  0.6 44.3 %copy-start = (f32[256,256]{1,0:T(8,128)S(1)}, f32[256,256]{1,0:T(8,128)}, u32[]{:S(2)}) copy-start(f32[256,256]{1,0:T(8,128)} %param.13) | copy-start | bytes 786436
  0.6 7.9 %copy-start.1 = (f32[256,256]{1,0:T(8,128)S(1)}, f32[256,256]{1,0:T(8,128)}, u32[]{:S(2)}) copy-start(f32[256,256]{1,0:T(8,128)} %refs_4_.1) | copy-start | bytes 786436
  8.5 3.3 copy-start.5
  13.3 7.7 %copy-start.8 = (f32[256,256]{1,0:T(8,128)S(1)}, f32[256,256]{1,0:T(8,128)}, u32[]{:S(2)}) copy-start(f32[256,256]{1,0:T(8,128)} %param.15) | copy-start | bytes 786436
  13.3 67.0 %all-to-all-start = ((f32[8,32,8,256]{3,2,1,0:T(8,128)}), f32[8,32,8,256]{3,2,1,0:T(8,128)}, u32[]{:S(2)}, u32[]{:S(2)}) async-start(f32[8,32,8,256]{3,2,1,0:T(8,128)} %bitcast.295), calls=%async_computation | async-start | bytes 4194304 | tf_op jit(solution)/shard_map/all_to_all | solution.py:97
  34.6 10.4 %copy-start.18 = (f32[256]{0:T(256)S(1)}, f32[256]{0:T(256)}, u32[]{:S(2)}) copy-start(f32[256]{0:T(256)} %param.17) | copy-start | bytes 3076
  34.6 10.4 %copy-start.19 = (f32[256]{0:T(256)S(1)}, f32[256]{0:T(256)}, u32[]{:S(2)}) copy-start(f32[256]{0:T(256)} %param.16) | copy-start | bytes 3076
  34.6 10.7 %copy-start.21 = (f32[256]{0:T(256)S(1)}, f32[256]{0:T(256)}, u32[]{:S(2)}) copy-start(f32[256]{0:T(256)} %param.18) | copy-start | bytes 3076
  45.4 3.4 copy-start.2
  80.3 6.1 %copy-start.20 = (f32[4]{0:T(128)S(1)}, f32[4]{0:T(128)}, u32[]{:S(2)}) copy-start(f32[4]{0:T(128)} %param.12) | copy-start | bytes 52
  80.3 65.0 %all-to-all-start.1 = ((f32[8,40,8,256]{3,2,1,0:T(8,128)}), f32[8,40,8,256]{3,2,1,0:T(8,128)S(1)}, u32[]{:S(2)}, u32[]{:S(2)}) async-start(f32[8,40,8,256]{3,2,1,0:T(8,128)} %pad_maximum_fusion), calls=%async_computation.1 | async-start | bytes 5242880 | tf_op jit(solution)/shard_map/all_to_all | solution.py:97
  146.1 6.2 %collective-permute-start = (f32[32,256]{1,0:T(8,128)S(1)}, f32[32,256]{1,0:T(8,128)S(1)}, u32[]{:S(2)}, u32[]{:S(2)}) collective-permute-start(f32[32,256]{1,0:T(8,128)S(1)} %slice.124), channel_id=1, source_target_pairs={{8,0},{16,8},{24,16},{0,24},{9,1},{17,9},{25,17},{1,25},{10,2},{18... | collective-permute-start | bytes 98312 | tf_op jit(solution)/shard_map/ppermute | solution.py:88
  153.9 59.4 %all-to-all-start.2 = ((f32[8,36,8,256]{3,2,1,0:T(8,128)}), f32[8,36,8,256]{3,2,1,0:T(8,128)}, u32[]{:S(2)}, u32[]{:S(2)}) async-start(f32[8,36,8,256]{3,2,1,0:T(8,128)} %pad_maximum_fusion.1), calls=%async_computation.2 | async-start | bytes 4718592 | tf_op jit(solution)/shard_map/all_to_all | solution.py:97
  216.2 52.3 %all-to-all-start.3 = ((f32[8,32,8,256]{3,2,1,0:T(8,128)}), f32[8,32,8,256]{3,2,1,0:T(8,128)}, u32[]{:S(2)}, u32[]{:S(2)}) async-start(f32[8,32,8,256]{3,2,1,0:T(8,128)} %bitcast.303), calls=%async_computation.3 | async-start | bytes 4194304 | tf_op jit(solution)/shard_map/all_to_all | solution.py:97
  220.5 3.8 copy-start.16
  225.4 11.9 %copy-start.22 = (f32[256]{0:T(256)S(1)}, f32[256]{0:T(256)}, u32[]{:S(2)}) copy-start(f32[256]{0:T(256)} %param.18) | copy-start | bytes 3076
  226.8 3.3 collective-permute-start.1
  226.8 3.6 collective-permute-start.2
  228.2 2.8 collective-permute-start.3
  229.7 6.2 %collective-permute-start.4 = (f32[256,256]{0,1:T(8,128)S(1)}, f32[256,256]{0,1:T(8,128)S(1)}, u32[]{:S(2)}, u32[]{:S(2)}) collective-permute-start(f32[256,256]{0,1:T(8,128)S(1)} %get-tuple-element.53), channel_id=1, source_target_pairs={{24,0},{0,8},{8,16},{16,24},{25,1},{1,9},{9,17},{17,25},{26,2},{2,... | collective-permute-start | bytes 786440 | tf_op jit(solution)/shard_map/ppermute | solution.py:88
  242.3 1.4 copy-start.12
  272.7 52.2 %all-to-all-start.4 = ((f32[8,32,8,256]{3,2,1,0:T(8,128)}), f32[8,32,8,256]{3,2,1,0:T(8,128)}, u32[]{:S(2)}, u32[]{:S(2)}) async-start(f32[8,32,8,256]{3,2,1,0:T(8,128)} %copy.55), calls=%async_computation.4 | async-start | bytes 4194304 | tf_op jit(solution)/shard_map/all_to_all | solution.py:97
  280.7 1.3 copy-start.14
  327.5 52.1 %all-to-all-start.5 = ((f32[8,32,8,256]{3,2,1,0:T(8,128)}), f32[8,32,8,256]{3,2,1,0:T(8,128)S(1)}, u32[]{:S(2)}, u32[]{:S(2)}) async-start(f32[8,32,8,256]{3,2,1,0:T(8,128)} %copy.59), calls=%async_computation.5 | async-start | bytes 4194304 | tf_op jit(solution)/shard_map/all_to_all | solution.py:97
  331.2 2.2 copy-start.15
  333.5 1.6 copy-start.13
  345.8 3.4 copy-start.11
  347.0 3.4 collective-permute-start.5
  379.5 1.4 copy-start.9
  380.9 57.7 %all-to-all-start.6 = ((f32[8,36,8,256]{3,2,1,0:T(8,128)}), f32[8,36,8,256]{3,2,1,0:T(8,128)S(1)}, u32[]{:S(2)}, u32[]{:S(2)}) async-start(f32[8,36,8,256]{3,2,1,0:T(8,128)} %pad_maximum_fusion.2), calls=%async_computation.6 | async-start | bytes 4718592 | tf_op jit(solution)/shard_map/all_to_all | solution.py:97
  438.6 5.0 copy-start.6
  443.6 52.2 %all-to-all-start.7 = ((f32[8,32,8,256]{3,2,1,0:T(8,128)}), f32[8,32,8,256]{3,2,1,0:T(8,128)}, u32[]{:S(2)}, u32[]{:S(2)}) async-start(f32[8,32,8,256]{3,2,1,0:T(8,128)} %copy.72), calls=%async_computation.7 | async-start | bytes 4194304 | tf_op jit(solution)/shard_map/all_to_all | solution.py:97
  450.6 1.6 copy-start.10
  457.7 9.6 %copy-start.7 = (f32[8,36,8,256]{3,2,1,0:T(8,128)S(1)}, f32[8,36,8,256]{3,2,1,0:T(8,128)}, u32[]{:S(2)}) copy-start(f32[8,36,8,256]{3,2,1,0:T(8,128)} %copy-done.6) | copy-start | bytes 7077892
  463.8 6.7 %collective-permute-start.6 = (f32[2,128]{1,0:T(2,128)S(1)}, f32[2,128]{1,0:T(2,128)S(1)}, u32[]{:S(2)}, u32[]{:S(2)}) collective-permute-start(f32[2,128]{1,0:T(2,128)S(1)} %broadcast_in_dim.36), channel_id=1, source_target_pairs={{24,0},{0,8},{8,16},{16,24},{25,1},{1,9},{9,17},{17,25},{26,2},{2,... | collective-permute-start | bytes 3080 | tf_op jit(solution)/shard_map/ppermute | solution.py:88
  463.8 6.7 %collective-permute-start.7 = (f32[2,128]{1,0:T(2,128)S(1)}, f32[2,128]{1,0:T(2,128)S(1)}, u32[]{:S(2)}, u32[]{:S(2)}) collective-permute-start(f32[2,128]{1,0:T(2,128)S(1)} %broadcast_in_dim.36), channel_id=1, source_target_pairs={{16,0},{24,8},{0,16},{8,24},{17,1},{25,9},{1,17},{9,25},{18,2},{26... | collective-permute-start | bytes 3080 | tf_op jit(solution)/shard_map/ppermute | solution.py:88
  465.6 4.9 collective-permute-start.8
  468.9 3.5 copy-start.17
  498.4 1.6 copy-start.3
  498.4 2.2 copy-start.4

commit v3 on v2

--- a/solution.py
+++ b/solution.py
@@ -1,6 +1,7 @@
 import jax
 import jax.numpy as jnp
 from jax import lax
+from jax.experimental.layout import Layout, with_layout_constraint
 from jax.experimental import pallas as pl
 from jax.experimental.pallas import tpu as pltpu
 from jax.sharding import PartitionSpec as P
@@ -22,8 +23,8 @@
 def edge_kernel(part_ref, basis_ref, pair_ref, eigen_ref, first_ref, last_ref, out_ref):
     top, low = split(basis_ref[...])
     right = jnp.concatenate([top, low, top], axis=0)
-    for at in range(part_ref.shape[0]):
-        top, low = split(part_ref[at])
+    for at in range(part_ref.shape[1]):
+        top, low = split(part_ref[:, at, :])
         left = jnp.concatenate([top, top, low], axis=0)
         hat = lax.dot_general(left, right, (((0,), (0,)), ((), ())), preferred_element_type=F32)
         modes = hat / (pair_ref[at : at + 1, :] + eigen_ref[...])
@@ -33,7 +34,7 @@
 
 
 def partial_edges(part, basis_rows, pair, eigen, first, last):
-    width, rows, depth = part.shape
+    rows, width, depth = part.shape
     block = 8
     whole = lambda j: (0, 0)
     return pl.pallas_call(
@@ -41,7 +42,7 @@
         out_shape=jax.ShapeDtypeStruct((width, 2 * width), F32),
         grid=(width // block,),
         in_specs=[
-            pl.BlockSpec((block, rows, depth), lambda j: (j, 0, 0)),
+            pl.BlockSpec((rows, block, depth), lambda j: (0, j, 0)),
             pl.BlockSpec((rows, width), whole),
             pl.BlockSpec((block, width), lambda j: (j, 0)),
             pl.BlockSpec((depth, width), whole),
@@ -93,6 +94,7 @@
     if extra is not None:
         blocks = jnp.concatenate([blocks, extra], axis=1)
     if before:
+        blocks = with_layout_constraint(blocks, Layout(major_to_minor=(0, 1, 2, 3)))
         blocks, _ = lax.optimization_barrier((blocks, before[-1]))
     got = lax.all_to_all(blocks, "slab", split_axis=0, concat_axis=0, tiled=True)
     before.append(got)
@@ -144,7 +146,7 @@
     lines = [outward(0)[0]]
 
     early = jnp.einsum("xyz,zk->xyk", field + coarse[0, 0], basis_z, precision=MID)
-    early = jnp.einsum("xyk,yj->jxk", early, basis_y, precision=MID)
+    early = jnp.einsum("xyk,yj->xjk", early, basis_y, precision=MID)
     spread_out = lambda column: jnp.broadcast_to(column[:, None], (width, width))
     share = partial_edges(
         early,

time: 513 us -> 512 us (level)
  Pallas kernels: 30.3 us -> 55.1 us
  local copies, waits for them, and re-layouts: 51.1 us -> 36.3 us
  waiting for transfers between devices: 271 us -> 264 us
    pallas_call x1, Pallas kernels: 23.4 us -> 48.2 us  [partial_edges(): pl.pallas_call(edge_kernel, out_shape=jax.ShapeDtypeStruct((width, 2 * wi...]
    optimization_barrier x3 -> x0, local copies, waits for them, and re-layouts: 11.8 us -> none  [exchange(): blocks, _ = lax.optimization_barrier((blocks, before[-1]))]
    all_to_all x8, waiting for transfers between devices: 268 us -> 261 us  [exchange(): lax.all_to_all(blocks, 'slab', split_axis=0, concat_axis=0, tiled=True)]
    dot_general x1 -> x4, local copies, waits for them, and re-layouts: 10.3 us -> 8.87 us  [modal(): spread = jnp.einsum('ijk,xi->xjk', modes, basis_x, precision=MID)]
    unnamed x47 -> x45, local copies, waits for them, and re-layouts: 12.2 us -> 11.8 us
  transfers between devices with their start and end apart: 17 -> 17, of which waited for: 10 -> 10; matrix products, arithmetic and copies ran while one was open for 22% -> 20% of each run, Pallas kernels for 5% -> 10%
where the time goes in v3:
time: 512 us; the launch traced here: 507 us
  waiting for transfers between devices  264 us (52%)
  matrix products  88.4 us (17%)
  Pallas kernels  55.1 us (11%)
  starting transfers between devices  47.8 us (9%)
  local copies, waits for them, and re-layouts  36.3 us (7%)
  other arithmetic  9.54 us (2%)
  between operations  5.56 us (1%)
    all_to_all x8, waiting for transfers between devices, exchange(): lax.all_to_all(blocks, 'slab', split_axis=0, concat_axis=0, tiled=True)  261 us
    pallas_call x1, Pallas kernels, partial_edges(): pl.pallas_call(edge_kernel, out_shape=jax.ShapeDtypeStruct((width, 2 * wi...  48.2 us
    all_to_all x8, starting transfers between devices, exchange(): lax.all_to_all(blocks, 'slab', split_axis=0, concat_axis=0, tiled=True)  39 us
    dot_general x4, matrix products, outward(): jnp.einsum('xyk,yj->xjk', part, basis_y[:, c * piece:(c + 1) * piece], pr...  20.8 us
    dot_general x4, matrix products, modal(): hat = jnp.einsum('xjk,xi->ijk', lines[c], basis_x, precision=MID)  17 us
    unnamed x45, local copies, waits for them, and re-layouts  11.8 us
  transfers between devices with their start and end apart: 17, of which 10 were waited for; matrix products, arithmetic and copies ran while one was open for 20% of the time, Pallas kernels for 10%

profile of v3, /device:TPU:0, one launch (start us, length us, event | category | flops | bytes accessed | tf_op | source)
XLA Modules:
  0.0 506.8 jit_solution(2780240705299562861)
XLA Ops:
  0.7 7.9 %fusion.1 = f32[32,256,256]{2,1,0:T(8,128)S(1)} fusion(f32[1,32,256,256]{3,2,1,0:T(8,128)} %param.10, f32[2,1,32,256,256]{4,3,2,1,0:T(8,128)} %param.11, f32[256,256]{1,0:T(8,128)} %param.15), kind=kOutput, calls=%fused_computation.3 | convolution fusion | flops 3223322624 | bytes 25427968 | tf_op jit(solution)/shard_map/xyz,zk->xyk/dot_general | solution.py:138
  8.6 2.7 convolution_bitcast_fusion.4
  11.9 1.5 copy.130
  13.5 7.7 %all-to-all-start = ((f32[8,32,8,256]{3,2,1,0:T(8,128)}), f32[8,32,8,256]{3,2,1,0:T(8,128)}, u32[]{:S(2)}, u32[]{:S(2)}) async-start(f32[8,32,8,256]{3,2,1,0:T(8,128)} %bitcast.296), calls=%async_computation | async-start | bytes 4194304 | tf_op jit(solution)/shard_map/all_to_all | solution.py:99
  21.4 7.9 %fusion = f32[32,256,256]{1,2,0:T(8,128)S(1)} fusion(f32[1,32,256,256]{3,2,1,0:T(8,128)} %param.10, f32[2,1,32,256,256]{4,3,2,1,0:T(8,128)} %param.11, f32[256,256]{1,0:T(8,128)S(1)} %copy-done.7), kind=kOutput, calls=%fused_computation.1 | convolution fusion | flops 3223322624 | bytes 25427968 | tf_op jit(solution)/shard_map/xyz,zk->xyk/dot_general | solution.py:148
  29.3 3.8 convolution_bitcast_fusion.part_ref
  33.4 48.2 %partial_edges.1 = f32[256,512]{1,0:T(8,128)S(1)} custom-call(f32[32,256,256]{2,1,0:T(8,128)S(1)} %convolution_bitcast_fusion.part_ref, f32[32,256]{1,0:T(8,128)S(1)} %constant_dynamic-slice_fusion.basis_ref, f32[256,256]{1,0:T(8,128)S(1)} %broadcast_add_fusion.pair_ref, f32[256,256]{1,0:T(8,128)S(1)} %broadcast_in_dim.26.eigen_ref, ...), custom_call_target="tpu_custom_call" | custom-call | flops 3221225472 | bytes 8388608 | tf_op jit(solution)/shard_map/partial_edges/pallas_call | solution.py:40
  81.7 6.1 %convolution_bitcast_fusion.2 = f32[32,8,8,256]{3,2,1,0:T(8,128)S(1)} fusion(f32[32,256,256]{2,1,0:T(8,128)} %copy-done.4, f32[256,256]{1,0:T(8,128)S(1)} %copy-done.1), kind=kOutput, calls=%fused_computation.41 | convolution fusion | flops 805306368 | bytes 10616832 | tf_op jit(solution)/shard_map/xyk,yj->xjk/dot_general | solution.py:141
  87.9 1.7 pad_maximum_fusion
  89.6 6.1 %all-to-all-start.1 = ((f32[8,40,8,256]{3,2,1,0:T(8,128)}), f32[8,40,8,256]{3,2,1,0:T(8,128)S(1)}, u32[]{:S(2)}, u32[]{:S(2)}) async-start(f32[8,40,8,256]{3,2,1,0:T(8,128)} %pad_maximum_fusion), calls=%async_computation.1 | async-start | bytes 5242880 | tf_op jit(solution)/shard_map/all_to_all | solution.py:99
  96.3 58.3 %all-to-all-done.1 = f32[8,40,8,256]{3,2,1,0:T(8,128)S(1)} async-done(((f32[8,40,8,256]{3,2,1,0:T(8,128)}), f32[8,40,8,256]{3,2,1,0:T(8,128)S(1)}, u32[]{:S(2)}, u32[]{:S(2)}) %all-to-all-start.1) | async-done | bytes 2621472 | tf_op jit(solution)/shard_map/all_to_all | solution.py:99
  155.7 6.0 %convolution_bitcast_fusion.3 = f32[32,8,8,256]{3,2,1,0:T(8,128)S(1)} fusion(f32[32,256,256]{2,1,0:T(8,128)} %copy-done.4, f32[256,256]{1,0:T(8,128)S(1)} %copy-done.1), kind=kOutput, calls=%fused_computation.42 | convolution fusion | flops 805306368 | bytes 10616832 | tf_op jit(solution)/shard_map/xyk,yj->xjk/dot_general | solution.py:141
  161.9 1.6 pad_maximum_fusion.1
  163.5 4.7 all-to-all-start.2
  169.5 6.1 %convolution_bitcast_fusion.1 = f32[32,8,8,256]{3,2,1,0:T(8,128)S(1)} fusion(f32[32,256,256]{2,1,0:T(8,128)} %copy-done.4, f32[256,256]{1,0:T(8,128)S(1)} %copy-done.1), kind=kOutput, calls=%fused_computation.40 | convolution fusion | flops 805306368 | bytes 10616832 | tf_op jit(solution)/shard_map/xyk,yj->xjk/dot_general | solution.py:141
  177.2 45.5 %all-to-all-done.2 = f32[8,36,8,256]{3,2,1,0:T(8,128)} async-done(((f32[8,36,8,256]{3,2,1,0:T(8,128)}), f32[8,36,8,256]{3,2,1,0:T(8,128)}, u32[]{:S(2)}, u32[]{:S(2)}) %all-to-all-start.2) | async-done | bytes 2359328 | tf_op jit(solution)/shard_map/all_to_all | solution.py:99
  225.6 4.4 all-to-all-start.3
  229.9 1.6 fusion.75
  231.6 1.5 fusion.31
  243.1 2.3 collective-permute-done.4
  246.7 5.0 fusion.13
  254.2 2.5 copy.52
  256.7 21.1 %all-to-all-done.3 = f32[8,32,8,256]{3,2,1,0:T(8,128)} async-done(((f32[8,32,8,256]{3,2,1,0:T(8,128)}), f32[8,32,8,256]{3,2,1,0:T(8,128)}, u32[]{:S(2)}, u32[]{:S(2)}) %all-to-all-start.3) | async-done | bytes 2097184 | tf_op jit(solution)/shard_map/all_to_all | solution.py:99
  277.8 4.4 all-to-all-start.4
  282.3 3.5 fusion.11
  288.3 2.5 copy.58
  290.8 39.1 %all-to-all-done.4 = f32[8,32,8,256]{3,2,1,0:T(8,128)} async-done(((f32[8,32,8,256]{3,2,1,0:T(8,128)}), f32[8,32,8,256]{3,2,1,0:T(8,128)}, u32[]{:S(2)}, u32[]{:S(2)}) %all-to-all-start.4) | async-done | bytes 2097184 | tf_op jit(solution)/shard_map/all_to_all | solution.py:99
  329.9 3.8 all-to-all-start.5
  333.7 1.9 slice.131
  338.7 3.5 fusion.9
  343.2 5.0 fusion.7
  354.7 1.6 pad_maximum_fusion.2
  356.3 25.9 %all-to-all-done.5 = f32[8,32,8,256]{3,2,1,0:T(8,128)S(1)} async-done(((f32[8,32,8,256]{3,2,1,0:T(8,128)}), f32[8,32,8,256]{3,2,1,0:T(8,128)S(1)}, u32[]{:S(2)}, u32[]{:S(2)}) %all-to-all-start.5) | async-done | bytes 2097184 | tf_op jit(solution)/shard_map/all_to_all | solution.py:99
  383.6 3.6 all-to-all-start.6
  387.2 2.6 convolution_bitcast_fusion.7
  389.8 2.6 copy.71
  392.4 48.8 %all-to-all-done.6 = f32[8,36,8,256]{3,2,1,0:T(8,128)S(1)} async-done(((f32[8,36,8,256]{3,2,1,0:T(8,128)}), f32[8,36,8,256]{3,2,1,0:T(8,128)S(1)}, u32[]{:S(2)}, u32[]{:S(2)}) %all-to-all-start.6) | async-done | bytes 2359328 | tf_op jit(solution)/shard_map/all_to_all | solution.py:99
  442.6 4.4 all-to-all-start.7
  447.0 2.6 convolution_bitcast_fusion.11
  452.3 1.6 copy.125
  457.1 1.7 fusion.30
  459.5 2.0 fusion.36
  462.9 1.9 collective-permute-start.7
  464.8 1.7 collective-permute-start.8
  468.2 1.6 copy.124
  472.5 22.3 %all-to-all-done.7 = f32[8,32,8,256]{3,2,1,0:T(8,128)} async-done(((f32[8,32,8,256]{3,2,1,0:T(8,128)}), f32[8,32,8,256]{3,2,1,0:T(8,128)}, u32[]{:S(2)}, u32[]{:S(2)}) %all-to-all-start.7) | async-done | bytes 2097184 | tf_op jit(solution)/shard_map/all_to_all | solution.py:99
  494.8 2.6 convolution_bitcast_fusion.6
  499.7 6.9 %last_product.1 = f32[32,256,256]{2,1,0:T(8,128)} custom-call(f32[32,64,256]{2,1,0:T(8,128)S(1)} %bitcast.298, f32[32,64,256]{2,1,0:T(8,128)S(1)} %bitcast.299, f32[32,64,256]{2,1,0:T(8,128)S(1)} %bitcast.300, f32[32,64,256]{2,1,0:T(8,128)S(1)} %bitcast.301, f32[256,256]{1,0:T(8,128)S(1)} %copy-done.1), custom_call_target="tpu_custom_call" | custom-call | tf_op jit(solution)/shard_map/last_product/pallas_call | solution.py:75
  (128 shorter events, 49.1 us)
Async XLA Ops:
  0.6 20.5 %copy-start = (f32[256,256]{1,0:T(8,128)S(1)}, f32[256,256]{1,0:T(8,128)}, u32[]{:S(2)}) copy-start(f32[256,256]{1,0:T(8,128)} %param.13) | copy-start | bytes 786436
  0.6 7.9 %copy-start.1 = (f32[256,256]{1,0:T(8,128)S(1)}, f32[256,256]{1,0:T(8,128)}, u32[]{:S(2)}) copy-start(f32[256,256]{1,0:T(8,128)} %refs_4_.1) | copy-start | bytes 786436
  8.5 3.4 copy-start.4
  13.5 7.7 %copy-start.7 = (f32[256,256]{1,0:T(8,128)S(1)}, f32[256,256]{1,0:T(8,128)}, u32[]{:S(2)}) copy-start(f32[256,256]{1,0:T(8,128)} %param.15) | copy-start | bytes 786436
  13.5 7.7 %copy-start.17 = (f32[256]{0:T(256)S(1)}, f32[256]{0:T(256)}, u32[]{:S(2)}) copy-start(f32[256]{0:T(256)} %param.17) | copy-start | bytes 3076
  13.5 7.7 %copy-start.18 = (f32[256]{0:T(256)S(1)}, f32[256]{0:T(256)}, u32[]{:S(2)}) copy-start(f32[256]{0:T(256)} %param.16) | copy-start | bytes 3076
  13.5 76.1 %all-to-all-start = ((f32[8,32,8,256]{3,2,1,0:T(8,128)}), f32[8,32,8,256]{3,2,1,0:T(8,128)}, u32[]{:S(2)}, u32[]{:S(2)}) async-start(f32[8,32,8,256]{3,2,1,0:T(8,128)} %bitcast.296), calls=%async_computation | async-start | bytes 4194304 | tf_op jit(solution)/shard_map/all_to_all | solution.py:99
  29.2 4.0 copy-start.20
  89.6 6.1 %copy-start.19 = (f32[4]{0:T(128)S(1)}, f32[4]{0:T(128)}, u32[]{:S(2)}) copy-start(f32[4]{0:T(128)} %param.12) | copy-start | bytes 52
  89.6 65.0 %all-to-all-start.1 = ((f32[8,40,8,256]{3,2,1,0:T(8,128)}), f32[8,40,8,256]{3,2,1,0:T(8,128)S(1)}, u32[]{:S(2)}, u32[]{:S(2)}) async-start(f32[8,40,8,256]{3,2,1,0:T(8,128)} %pad_maximum_fusion), calls=%async_computation.1 | async-start | bytes 5242880 | tf_op jit(solution)/shard_map/all_to_all | solution.py:99
  155.4 6.4 %collective-permute-start = (f32[32,256]{1,0:T(8,128)S(1)}, f32[32,256]{1,0:T(8,128)S(1)}, u32[]{:S(2)}, u32[]{:S(2)}) collective-permute-start(f32[32,256]{1,0:T(8,128)S(1)} %slice.124), channel_id=1, source_target_pairs={{8,0},{16,8},{24,16},{0,24},{9,1},{17,9},{25,17},{1,25},{10,2},{18... | collective-permute-start | bytes 98312 | tf_op jit(solution)/shard_map/ppermute | solution.py:89
  163.5 59.2 %all-to-all-start.2 = ((f32[8,36,8,256]{3,2,1,0:T(8,128)}), f32[8,36,8,256]{3,2,1,0:T(8,128)}, u32[]{:S(2)}, u32[]{:S(2)}) async-start(f32[8,36,8,256]{3,2,1,0:T(8,128)} %pad_maximum_fusion.1), calls=%async_computation.2 | async-start | bytes 4718592 | tf_op jit(solution)/shard_map/all_to_all | solution.py:99
  225.6 52.2 %all-to-all-start.3 = ((f32[8,32,8,256]{3,2,1,0:T(8,128)}), f32[8,32,8,256]{3,2,1,0:T(8,128)}, u32[]{:S(2)}, u32[]{:S(2)}) async-start(f32[8,32,8,256]{3,2,1,0:T(8,128)} %bitcast.303), calls=%async_computation.3 | async-start | bytes 4194304 | tf_op jit(solution)/shard_map/all_to_all | solution.py:99
  229.9 3.8 copy-start.15
  234.7 12.0 %copy-start.21 = (f32[256]{0:T(256)S(1)}, f32[256]{0:T(256)}, u32[]{:S(2)}) copy-start(f32[256]{0:T(256)} %param.18) | copy-start | bytes 3076
  236.2 3.4 collective-permute-start.1
  236.2 3.6 collective-permute-start.2
  237.7 2.8 collective-permute-start.3
  239.2 6.2 %collective-permute-start.4 = (f32[256,256]{0,1:T(8,128)S(1)}, f32[256,256]{0,1:T(8,128)S(1)}, u32[]{:S(2)}, u32[]{:S(2)}) collective-permute-start(f32[256,256]{0,1:T(8,128)S(1)} %get-tuple-element.53), channel_id=1, source_target_pairs={{24,0},{0,8},{8,16},{16,24},{25,1},{1,9},{9,17},{17,25},{26,2},{2,... | collective-permute-start | bytes 786440 | tf_op jit(solution)/shard_map/ppermute | solution.py:89
  251.8 1.4 copy-start.11
  277.8 52.2 %all-to-all-start.4 = ((f32[8,32,8,256]{3,2,1,0:T(8,128)}), f32[8,32,8,256]{3,2,1,0:T(8,128)}, u32[]{:S(2)}, u32[]{:S(2)}) async-start(f32[8,32,8,256]{3,2,1,0:T(8,128)} %bitcast.306), calls=%async_computation.4 | async-start | bytes 4194304 | tf_op jit(solution)/shard_map/all_to_all | solution.py:99
  285.8 1.4 copy-start.13
  329.9 52.2 %all-to-all-start.5 = ((f32[8,32,8,256]{3,2,1,0:T(8,128)}), f32[8,32,8,256]{3,2,1,0:T(8,128)S(1)}, u32[]{:S(2)}, u32[]{:S(2)}) async-start(f32[8,32,8,256]{3,2,1,0:T(8,128)} %bitcast.305), calls=%async_computation.5 | async-start | bytes 4194304 | tf_op jit(solution)/shard_map/all_to_all | solution.py:99
  333.7 2.2 copy-start.14
  336.0 1.6 copy-start.12
  348.2 1.4 copy-start.10
  350.8 3.8 collective-permute-start.5
  382.2 1.4 copy-start.8
  383.6 57.7 %all-to-all-start.6 = ((f32[8,36,8,256]{3,2,1,0:T(8,128)}), f32[8,36,8,256]{3,2,1,0:T(8,128)S(1)}, u32[]{:S(2)}, u32[]{:S(2)}) async-start(f32[8,36,8,256]{3,2,1,0:T(8,128)} %pad_maximum_fusion.2), calls=%async_computation.6 | async-start | bytes 4718592 | tf_op jit(solution)/shard_map/all_to_all | solution.py:99
  441.2 1.4 copy-start.5
  442.6 52.2 %all-to-all-start.7 = ((f32[8,32,8,256]{3,2,1,0:T(8,128)}), f32[8,32,8,256]{3,2,1,0:T(8,128)}, u32[]{:S(2)}, u32[]{:S(2)}) async-start(f32[8,32,8,256]{3,2,1,0:T(8,128)} %bitcast.304), calls=%async_computation.7 | async-start | bytes 4194304 | tf_op jit(solution)/shard_map/all_to_all | solution.py:99
  449.6 1.6 copy-start.9
  456.7 9.8 %copy-start.6 = (f32[8,36,8,256]{3,2,1,0:T(8,128)S(1)}, f32[8,36,8,256]{3,2,1,0:T(8,128)}, u32[]{:S(2)}) copy-start(f32[8,36,8,256]{3,2,1,0:T(8,128)} %copy-done.5) | copy-start | bytes 7077892
  462.9 6.9 %collective-permute-start.6 = (f32[2,128]{1,0:T(2,128)S(1)}, f32[2,128]{1,0:T(2,128)S(1)}, u32[]{:S(2)}, u32[]{:S(2)}) collective-permute-start(f32[2,128]{1,0:T(2,128)S(1)} %broadcast_in_dim.36), channel_id=1, source_target_pairs={{24,0},{0,8},{8,16},{16,24},{25,1},{1,9},{9,17},{17,25},{26,2},{2,... | collective-permute-start | bytes 3080 | tf_op jit(solution)/shard_map/ppermute | solution.py:89
  462.9 6.9 %collective-permute-start.7 = (f32[2,128]{1,0:T(2,128)S(1)}, f32[2,128]{1,0:T(2,128)S(1)}, u32[]{:S(2)}, u32[]{:S(2)}) collective-permute-start(f32[2,128]{1,0:T(2,128)S(1)} %broadcast_in_dim.36), channel_id=1, source_target_pairs={{16,0},{24,8},{0,16},{8,24},{17,1},{25,9},{1,17},{9,25},{18,2},{26... | collective-permute-start | bytes 3080 | tf_op jit(solution)/shard_map/ppermute | solution.py:89
  464.8 4.9 collective-permute-start.8
  468.2 3.5 copy-start.16
  497.4 1.6 copy-start.2
  497.5 2.2 copy-start.3
